TPU v7x, 1024 devices: a whole 4x4x32 slice. The times are simulated.
1024 devices in a mesh: fsdp: 64 (over z, y_lo), rep: 4 (over x), dp: 4 (over y_hi, core).
Axes of the slice: x: 4, y: 4 (y_hi: 2, y_lo: 2; y = y_hi * 2 + y_lo), z: 32, core: 2. Of those that a mesh axis runs over, the one named last changes fastest.
Arguments:
- trainer_gate: bfloat16 [8192, 4, 4096], P('fsdp', 'dp'), may hold values from -0.0625 to 0.0625
- trainer_up: bfloat16 [8192, 4, 4096], P('fsdp', 'dp'), may hold values from -0.0625 to 0.0625
- owner_map: int32 [64], replicated, may hold values from 0 to 63, each once
- sketch_seeds: int32 [8192], replicated, may hold values from 0 to 1
- probes: bfloat16 [4, 64, 128, 8192], P('rep', 'fsdp'), may hold values from -6 to 6
Outputs:
- digest: float32 [2, 64, 4, 4096], P(None, None, 'dp', 'fsdp')
- hidden: bfloat16 [4, 64, 128, 4, 256], P('rep', 'fsdp', None, 'dp')
Inputs may be any that keep to these rules, and one draw needn't show every extreme that they name: owner_map is a permutation: every true row block is held at exactly one trainer position.
All inputs are finite; a program needn't handle non-finite values.
Results may differ from a plain program's by a relative error of at most 0.01.
Values may be sent and summed in bfloat16 or wider, within the bound.
No kernel may reach another device: no remote copies, remote signals or barrier semaphores. Data moves between devices by JAX's collectives and lax.ppermute only.
A program may use at most 64 MiB of HBM per device.

v0:
```python
import jax
import jax.numpy as jnp
from jax import lax
from jax.sharding import PartitionSpec as P


def on_device(trainer_gate, trainer_up, owner_map, sketch_seeds, probes):
    local_rows, local_dp, slice_width = trainer_gate.shape
    count_fsdp = lax.axis_size("fsdp")
    count_rep = lax.axis_size("rep")
    ranks = min(16, count_fsdp)
    subgroups = count_fsdp // ranks
    rank_width = slice_width // ranks
    narrow = rank_width // subgroups
    total_rows = local_rows * count_fsdp
    blocks_all = total_rows // 128
    local_blocks = local_rows // 128
    quarter = 128 // count_rep
    replica = lax.axis_index("rep")
    member = lax.axis_index("fsdp")
    subgroup = member % subgroups
    probe_rows = probes.shape[2]
    wide = probes.reshape(probe_rows, total_rows).astype(jnp.float32)
    meansq = jnp.mean(wide * wide, axis=-1, keepdims=True)
    normed = (wide / jnp.sqrt(meansq + 1e-05)).astype(jnp.bfloat16)

    def pick(matrix):
        viewed = matrix.reshape(local_blocks, count_rep, quarter, local_dp, ranks, 1, rank_width)
        chosen = lax.dynamic_slice_in_dim(viewed, replica, 1, 1)
        spread = jnp.broadcast_to(
            chosen, (local_blocks, 1, quarter, local_dp, ranks, subgroups, rank_width)
        )
        return spread.reshape(local_blocks * quarter, local_dp, count_fsdp * rank_width)

    gate_recv, up_recv = (
        lax.all_to_all(pick(trainer_gate), "fsdp", split_axis=2, concat_axis=0, tiled=True),
        lax.all_to_all(pick(trainer_up), "fsdp", split_axis=2, concat_axis=0, tiled=True),
    )
    positions = jnp.arange(blocks_all, dtype=jnp.int32)
    inverse = jnp.sum(
        jnp.where(owner_map[None, :] == positions[:, None], positions[None, :], 0), axis=1
    )

    def restore(matrix):
        return matrix.reshape(blocks_all, quarter, local_dp, rank_width)[inverse]

    gate_mine = restore(gate_recv)
    up_mine = restore(up_recv)
    all_signs = (1 - 2 * sketch_seeds).astype(jnp.float32).reshape(blocks_all, count_rep, quarter)

    def sketch(matrix, signs):
        part = lax.dynamic_slice_in_dim(matrix, subgroup * narrow, narrow, 3).astype(jnp.float32)
        return 8.0 * jnp.sum(signs[:, :, None, None] * part, axis=1)

    gate_full, up_full = (
        lax.all_gather(gate_mine, "rep", axis=1, tiled=True),
        lax.all_gather(up_mine, "rep", axis=1, tiled=True),
    )
    full_signs = all_signs.reshape(blocks_all, 128)
    digest = jnp.stack([sketch(gate_full, full_signs), sketch(up_full, full_signs)])
    gate_out = jnp.dot(
        normed,
        gate_full.reshape(total_rows, local_dp * rank_width),
        preferred_element_type=jnp.float32,
    )
    up_out = jnp.dot(
        normed,
        up_full.reshape(total_rows, local_dp * rank_width),
        preferred_element_type=jnp.float32,
    )
    hidden = (jax.nn.silu(gate_out) * up_out).astype(jnp.bfloat16)
    return (digest, hidden.reshape(1, 1, probe_rows, local_dp, rank_width))


def solution(mesh):
    placed = (P("fsdp", "dp", None), P("fsdp", "dp", None), P(), P(), P("rep", "fsdp", None, None))
    return jax.shard_map(
        on_device,
        mesh=mesh,
        in_specs=placed,
        out_specs=(P(None, None, "dp", "fsdp"), P("rep", "fsdp", None, "dp", None)),
        check_vma=False,
    )
```

profile of v0, /device:TPU:1, one launch (start us, length us, event | category | flops | bytes accessed | tf_op | source)
XLA Modules:
  0.0 493.8 jit_solution(11212213628898009137)
XLA Ops:
  7.2 1.5 copy.33
  8.6 1.5 copy.34
  10.7 0.8 broadcast_in_dim.38
  11.5 12.7 %copy.24 = bf16[32,1,16384]{0,1,2:T(2,128)(2,1)} copy(bf16[32,1,16384]{2,0,1:T(8,128)(2,1)S(1)} %broadcast_in_dim.38) | data formatting | bytes 2097152 | tf_op jit(solution)/shard_map/broadcast_in_dim | solution.py:30
  24.7 90.8 %reduce.3 = bf16[16384,32]{1,0:T(8,128)(2,1)} reduce(bf16[16384,1,32]{2,1,0:T(2,128)(2,1)} %bitcast.64, bf16[]{:T(256)} %broadcast.85), dimensions={1}, to_apply=%bitcast.52.reduce_sub_computation | reduce | bytes 2097154
  115.4 7.3 %reshape.138 = bf16[64,2,4096]{2,1,0:T(2,128)(2,1)} reshape(bf16[16384,32]{1,0:T(8,128)(2,1)} %reduce.3) | data formatting | bytes 2097152
  122.7 31.1 %all-to-all-start = ((bf16[64,2,4096]{2,1,0:T(2,128)(2,1)}), bf16[64,2,4096]{2,1,0:T(2,128)(2,1)S(1)}, u32[]{:S(2)}, u32[]{:S(2)}) async-start(bf16[64,2,4096]{2,1,0:T(2,128)(2,1)} %reshape.138), calls=%async_computation | async-start | bytes 2097152 | tf_op jit(solution)/shard_map/all_to_all | solution.py:36
  154.3 0.8 broadcast_in_dim.43
  155.1 12.7 %copy.27 = bf16[32,1,16384]{0,1,2:T(2,128)(2,1)} copy(bf16[32,1,16384]{2,0,1:T(8,128)(2,1)S(1)} %broadcast_in_dim.43) | data formatting | bytes 2097152 | tf_op jit(solution)/shard_map/broadcast_in_dim | solution.py:30
  167.8 90.8 %reduce.4 = bf16[16384,32]{1,0:T(8,128)(2,1)} reduce(bf16[16384,1,32]{2,1,0:T(2,128)(2,1)} %bitcast.65, bf16[]{:T(256)} %broadcast.85), dimensions={1}, to_apply=%bitcast.54.reduce_sub_computation | reduce | bytes 2097154
  258.5 7.3 %reshape.140 = bf16[64,2,4096]{2,1,0:T(2,128)(2,1)} reshape(bf16[16384,32]{1,0:T(8,128)(2,1)} %reduce.4) | data formatting | bytes 2097152
  265.8 22.5 %all-to-all-start.1 = ((bf16[64,2,4096]{2,1,0:T(2,128)(2,1)}), bf16[64,2,4096]{2,1,0:T(2,128)(2,1)S(1)}, u32[]{:S(2)}, u32[]{:S(2)}) async-start(bf16[64,2,4096]{2,1,0:T(2,128)(2,1)} %reshape.140), calls=%async_computation.1 | async-start | bytes 2097152 | tf_op jit(solution)/shard_map/all_to_all | solution.py:37
  288.5 14.1 %reshape.139 = bf16[16384,1,32]{2,1,0:T(2,128)(2,1)} reshape(bf16[64,2,4096]{2,1,0:T(2,128)(2,1)S(1)} %all-to-all-done) | data formatting | bytes 2097152
  302.6 15.1 %copy.25 = bf16[32,1,16384]{2,0,1:T(8,128)(2,1)S(1)} copy(bf16[32,1,16384]{0,1,2:T(2,128)(2,1)} %bitcast.66) | data formatting | bytes 2097152 | tf_op jit(solution)/shard_map/all_to_all | solution.py:36
  317.8 1.7 gather_fusion
  319.8 75.1 %all-to-all-done.1 = bf16[64,2,4096]{2,1,0:T(2,128)(2,1)S(1)} async-done(((bf16[64,2,4096]{2,1,0:T(2,128)(2,1)}), bf16[64,2,4096]{2,1,0:T(2,128)(2,1)S(1)}, u32[]{:S(2)}, u32[]{:S(2)}) %all-to-all-start.1) | async-done | bytes 1048608 | tf_op jit(solution)/shard_map/all_to_all | solution.py:37
  394.9 14.1 %reshape.141 = bf16[16384,1,32]{2,1,0:T(2,128)(2,1)} reshape(bf16[64,2,4096]{2,1,0:T(2,128)(2,1)S(1)} %all-to-all-done.1) | data formatting | bytes 2097152
  409.0 15.1 %copy.28 = bf16[32,1,16384]{2,0,1:T(8,128)(2,1)S(1)} copy(bf16[32,1,16384]{0,1,2:T(2,128)(2,1)} %bitcast.67) | data formatting | bytes 2097152 | tf_op jit(solution)/shard_map/all_to_all | solution.py:37
  424.1 1.2 copy.37
  425.3 2.8 gather_fusion.1
  428.6 2.1 fusion.4
  430.8 48.5 %all-gather.7.cloned.1.call-done = bf16[64,128,256]{2,1,0:T(8,128)(2,1)} async-done(((bf16[64,32,256]{2,1,0:T(8,128)(2,1)}), bf16[64,128,256]{2,1,0:T(8,128)(2,1)}) %all-gather.7.cloned.1.call-update) | async-done | bytes 4194320 | tf_op jit(solution)/shard_map/all_gather | solution.py:57
  479.3 4.1 fusion.3
  485.6 1.4 fusion.6
  (31 shorter events, 4.8 us)
Async XLA Ops:
  122.7 143.1 %all-to-all-start = ((bf16[64,2,4096]{2,1,0:T(2,128)(2,1)}), bf16[64,2,4096]{2,1,0:T(2,128)(2,1)S(1)}, u32[]{:S(2)}, u32[]{:S(2)}) async-start(bf16[64,2,4096]{2,1,0:T(2,128)(2,1)} %reshape.138), calls=%async_computation | async-start | bytes 2097152 | tf_op jit(solution)/shard_map/all_to_all | solution.py:36
  258.5 29.8 %copy-start.4 = (s32[64]{0:T(128)S(1)}, s32[64]{0:T(128)}, u32[]{:S(2)}) copy-start(s32[64]{0:T(128)} %param.7) | copy-start | bytes 772
  265.8 129.0 %all-to-all-start.1 = ((bf16[64,2,4096]{2,1,0:T(2,128)(2,1)}), bf16[64,2,4096]{2,1,0:T(2,128)(2,1)S(1)}, u32[]{:S(2)}, u32[]{:S(2)}) async-start(bf16[64,2,4096]{2,1,0:T(2,128)(2,1)} %reshape.140), calls=%async_computation.1 | async-start | bytes 2097152 | tf_op jit(solution)/shard_map/all_to_all | solution.py:37
  288.3 142.5 %all-gather.5.cloned.1.call-start = ((), (), s32[]{:S(2)}) async-start(), calls=%async_computation.2 | async-start | bytes 5242880 | tf_op jit(solution)/shard_map/all_gather | solution.py:56
  319.5 159.7 %all-gather.7.cloned.1.call-start = ((), (), s32[]{:S(2)}) async-start(), calls=%async_computation.3 | async-start | bytes 5242880 | tf_op jit(solution)/shard_map/all_gather | solution.py:57
  424.1 4.0 copy-start.2
  424.1 4.5 copy-start.3
  479.3 4.8 copy-start
  483.3 2.2 copy-start.1
Sparse Core Ops, SparseCore 0:
  319.7 66.8 all-gather.4
  428.2 50.9 all-gather.6
where the time goes:
time: 495 us; the launch traced here: 494 us
  other arithmetic  189 us (38%)
  waiting for transfers between devices  124 us (25%)
  local copies, waits for them, and re-layouts  111 us (22%)
  starting transfers between devices  53.8 us (11%)
  between operations  14.3 us (3%)
    unnamed x2, other arithmetic  182 us
    all_to_all x1, waiting for transfers between devices, on_device(): lax.all_to_all(pick(trainer_up), 'fsdp', split_axis=2, concat_axis=0, til...  75.1 us
    all_gather x1, waiting for transfers between devices, on_device(): lax.all_gather(up_mine, 'rep', axis=1, tiled=True)  48.5 us
    unnamed x17, local copies, waits for them, and re-layouts  46.9 us
    all_to_all x1, starting transfers between devices, on_device(): lax.all_to_all(pick(trainer_gate), 'fsdp', split_axis=2, concat_axis=0, t...  31.1 us
    broadcast_in_dim x7, local copies, waits for them, and re-layouts, pick(): jnp.broadcast_to(chosen, (local_blocks, 1, quarter, local_dp, ranks, subg...  28 us
    all_to_all x1, starting transfers between devices, on_device(): lax.all_to_all(pick(trainer_up), 'fsdp', split_axis=2, concat_axis=0, til...  22.5 us
    all_to_all x2, local copies, waits for them, and re-layouts, on_device(): lax.all_to_all(pick(trainer_up), 'fsdp', split_axis=2, concat_axis=0, til...  16.3 us
  transfers between devices with their start and end apart: 4, of which 2 were waited for; matrix products, arithmetic and copies ran while one was open for 36% of the time, Pallas kernels for 0%

commit v1 on v0

v1 whole, which is shorter than its diff:
```python
import jax
import jax.numpy as jnp
import numpy as np
from jax import lax
from jax.sharding import Mesh, PartitionSpec as P

FSDP = ("ft", "fs")


def on_device(trainer_gate, trainer_up, owner_map, sketch_seeds, probes):
    rows, _, width = trainer_gate.shape
    n_rep = lax.axis_size("rep")
    n_ft = lax.axis_size("ft")
    n_fs = lax.axis_size("fs")
    n_f = n_ft * n_fs
    total_rows = rows * n_f
    blocks_all = total_rows // 128
    rank_width = width // n_ft
    narrow = rank_width // n_fs
    quarter = 128 // n_rep
    piece = quarter // n_fs
    replica = lax.axis_index("rep")
    member = lax.axis_index("ft") * n_fs + lax.axis_index("fs")
    sub = lax.axis_index("fs")

    weights = jnp.stack([trainer_gate.reshape(rows, width), trainer_up.reshape(rows, width)])

    mine = lax.dynamic_slice_in_dim(weights, replica * quarter, quarter, 1)
    send = mine.reshape(2, n_fs, piece, n_ft, rank_width).transpose(3, 1, 2, 0, 4)
    send = send.reshape(n_f, piece, 2 * rank_width)
    recv = lax.all_to_all(send, FSDP, 0, 0, tiled=True)

    positions = jnp.arange(blocks_all, dtype=jnp.int32)
    true_block = owner_map[member]
    signs = (1 - 2 * sketch_seeds).astype(jnp.float32)
    own_signs = lax.dynamic_slice_in_dim(signs, true_block * 128, 128, 0)
    digest_row = 8.0 * jnp.einsum(
        "k,pkc->pc", own_signs.astype(jnp.bfloat16), weights, preferred_element_type=jnp.float32
    )
    digest_send = digest_row.reshape(2, n_f, narrow).transpose(1, 0, 2)
    digest_recv = lax.all_to_all(digest_send, FSDP, 0, 0, tiled=True)

    inverse = jnp.sum(
        jnp.where(owner_map[None, :] == positions[:, None], positions[None, :], 0), axis=1
    )
    digest = digest_recv[inverse].transpose(1, 0, 2).reshape(2, blocks_all, 1, narrow)

    probe_rows = probes.shape[2]
    wide = probes.reshape(probe_rows, total_rows).astype(jnp.float32)
    meansq = jnp.mean(wide * wide, axis=-1, keepdims=True)
    normed = (wide / jnp.sqrt(meansq + 1e-05)).astype(jnp.bfloat16)
    normed_send = normed.reshape(probe_rows, blocks_all, n_rep, quarter).transpose(2, 0, 1, 3)
    normed_send = normed_send.reshape(n_rep, probe_rows, blocks_all * quarter)
    normed_recv = lax.all_to_all(normed_send, "rep", 0, 0, tiled=True)

    gathered = lax.all_gather(recv, "fs", axis=0, tiled=False)
    ordered = jnp.take(gathered, inverse, axis=1).transpose(1, 0, 2, 3)
    ordered = ordered.reshape(blocks_all * quarter, 2 * rank_width)

    lhs = normed_recv.reshape(n_rep * probe_rows, blocks_all * quarter)
    partial = jnp.dot(lhs, ordered, preferred_element_type=jnp.float32)
    partial = partial.reshape(n_rep, probe_rows, 2 * rank_width)
    summed = lax.psum_scatter(partial, "rep", scatter_dimension=0, tiled=True)
    gate_out = summed[0, :, :rank_width]
    up_out = summed[0, :, rank_width:]
    hidden = (jax.nn.silu(gate_out) * up_out).astype(jnp.bfloat16)
    return (digest, hidden.reshape(1, 1, probe_rows, 1, rank_width))


def solution(mesh):
    n_fsdp = mesh.shape["fsdp"]
    n_ft = min(16, n_fsdp)
    devices = np.asarray(mesh.devices).reshape(
        n_ft, n_fsdp // n_ft, mesh.shape["rep"], mesh.shape["dp"]
    )
    split = Mesh(devices, ("ft", "fs", "rep", "dp"))
    placed = (P(FSDP, "dp", None), P(FSDP, "dp", None), P(), P(), P("rep", FSDP, None, None))
    return jax.shard_map(
        on_device,
        mesh=split,
        in_specs=placed,
        out_specs=(P(None, None, "dp", FSDP), P("rep", FSDP, None, "dp", None)),
        check_vma=False,
    )
```

time: 495 us -> 220 us (0.44)
  the two profiles are of different devices: /device:TPU:1 before, /device:TPU:2 now
where the time goes in v1:
time: 220 us
  blocking collectives  142 us (65%)
  waiting for transfers between devices  33 us (15%)
  between operations  14.8 us (7%)
  local copies, waits for them, and re-layouts  12.3 us (6%)
  other arithmetic  6.87 us (3%)
  matrix products  5.74 us (3%)
  starting transfers between devices  5.13 us (2%)
    all_to_all x1, blocking collectives, on_device(): recv = lax.all_to_all(send, FSDP, 0, 0, tiled=True)  95.2 us
    all_to_all x1, blocking collectives, on_device(): digest_recv = lax.all_to_all(digest_send, FSDP, 0, 0, tiled=True)  46.8 us
    all_gather x1, waiting for transfers between devices, on_device(): gathered = lax.all_gather(recv, 'fs', axis=0, tiled=False)  33 us
    all_to_all x1, starting transfers between devices, on_device(): normed_recv = lax.all_to_all(normed_send, 'rep', 0, 0, tiled=True)  5.09 us
    dot_general x1, matrix products, on_device(): partial = jnp.dot(lhs, ordered, preferred_element_type=jnp.float32)  4.61 us
  transfers between devices with their start and end apart: 3, of which 1 were waited for; matrix products, arithmetic and copies ran while one was open for 8% of the time, Pallas kernels for 0%

profile of v1, /device:TPU:2, one launch (start us, length us, event | category | flops | bytes accessed | tf_op | source)
XLA Modules:
  0.0 219.8 jit_solution(12316330838170785678)
XLA Ops:
  7.2 1.1 fusion.2
  8.3 0.5 copy.28
  8.8 0.3 reshape.113
  9.2 95.2 %all_to_all.15 = bf16[64,8,512]{2,1,0:T(8,128)(2,1)} all-to-all(bf16[64,8,512]{2,1,0:T(8,128)(2,1)S(1)} %reshape.113), channel_id=1, replica_groups=mesh['ft'=16,'fs'=4,'rep'=4,'dp'=4] {'ft','fs'}, dimensions={0} | all-to-all | bytes 1048576 | tf_op jit(solution)/shard_map/all_to_all | solution.py:31
  104.4 3.2 %copy.25 = bf16[1,1,128,8192]{2,3,1,0:T(8,128)(2,1)S(1)} copy(bf16[1,1,128,8192]{3,2,1,0:T(8,128)(2,1)} %param.9) | data formatting | bytes 4194304 | tf_op args[4]
  107.6 1.1 multiply_reduce_fusion
  108.7 0.6 fusion.1
  109.3 0.4 copy.26
  109.7 2.7 %copy.27 = bf16[4,128,2048]{2,1,0:T(8,128)(2,1)} copy(bf16[4,128,2048]{1,2,0:T(8,128)(2,1)S(1)} %bitcast.48) | data formatting | bytes 4194304 | tf_op jit(solution)/shard_map/reshape | solution.py:53
  112.4 5.1 %all-to-all-start.1 = ((bf16[4,128,2048]{2,1,0:T(8,128)(2,1)}), bf16[4,128,2048]{2,1,0:T(8,128)(2,1)}, u32[]{:S(2)}, u32[]{:S(2)}) async-start(bf16[4,128,2048]{2,1,0:T(8,128)(2,1)} %copy.27), calls=%async_computation.1 | async-start | bytes 4194304 | tf_op jit(solution)/shard_map/all_to_all | solution.py:54
  117.5 0.1 select_reduce_fusion
  117.6 33.0 %all-gather.3.cloned.1.call-done = bf16[256,8,512]{2,1,0:T(8,128)(2,1)} async-done(((bf16[64,8,512]{2,1,0:T(8,128)(2,1)}), bf16[256,8,512]{2,1,0:T(8,128)(2,1)}) %all-gather.3.cloned.1.call-update) | async-done | bytes 2097168 | tf_op jit(solution)/shard_map/all_gather | solution.py:56
  150.6 2.3 %gather_fusion.1 = bf16[64,4,8,512]{3,2,1,0:T(8,128)(2,1)S(1)} fusion(bf16[4,64,8,512]{3,2,1,0:T(8,128)(2,1)} %bitcast.49, s32[1024]{0:T(1024)S(1)} %pad_clamp_fusion), kind=kCustom, calls=%fused_computation.1 | custom fusion | bytes 4194560 | tf_op jit(solution)/shard_map/jit(_take)/gather | solution.py:57
  152.9 1.6 broadcast_select_fusion
  154.5 4.6 %fusion.16 = f32[4,128,512]{2,1,0:T(8,128)} fusion(bf16[4,128,2048]{2,1,0:T(8,128)(2,1)} %all-to-all-done.1, bf16[2048,512,1]{1,0,2:T(8,128)(2,1)} %bitcast.50), kind=kOutput, calls=%fused_computation.35 | convolution fusion | flops 1073741824 | bytes 5242880 | tf_op jit(solution)/shard_map/dot_general | solution.py:61
  159.2 0.6 dynamic_slice.9
  160.4 1.1 fusion
  161.8 0.1 reshape.136
  161.9 46.8 %all_to_all.16 = f32[64,1,128]{2,1,0:T(1,128)S(1)} all-to-all(f32[64,1,128]{2,1,0:T(1,128)S(1)} %reshape.136), channel_id=1, replica_groups=mesh['ft'=16,'fs'=4,'rep'=4,'dp'=4] {'ft','fs'}, dimensions={0} | all-to-all | bytes 65536 | tf_op jit(solution)/shard_map/all_to_all | solution.py:41
  208.6 0.5 broadcast.72
  209.2 0.7 reduce.1
  210.0 0.7 gather_fusion
  210.6 0.7 copy.29
  211.3 1.6 fusion.4
  (20 shorter events, 0.4 us)
Async XLA Ops:
  7.2 143.5 %all-gather.3.cloned.1.call-start = ((), (), s32[]{:S(2)}) async-start(), calls=%async_computation.5 | async-start | bytes 2621440 | tf_op jit(solution)/shard_map/all_gather | solution.py:56
  112.4 5.1 %copy-start.2 = (s32[64]{0:T(128)S(1)}, s32[64]{0:T(128)}, u32[]{:S(2)}) copy-start(s32[64]{0:T(128)} %param.7) | copy-start | bytes 772
  112.4 42.1 %all-to-all-start.1 = ((bf16[4,128,2048]{2,1,0:T(8,128)(2,1)}), bf16[4,128,2048]{2,1,0:T(8,128)(2,1)}, u32[]{:S(2)}, u32[]{:S(2)}) async-start(bf16[4,128,2048]{2,1,0:T(8,128)(2,1)} %copy.27), calls=%async_computation.1 | async-start | bytes 4194304 | tf_op jit(solution)/shard_map/all_to_all | solution.py:54
  117.5 93.8 %reduce-scatter.2.cloned.1.call-start = ((), (), s32[]{:S(2)}) async-start(), calls=%async_computation.4 | async-start | bytes 1310720 | tf_op jit(solution)/shard_map/reduce_scatter | solution.py:63
  154.5 5.9 %copy-start = (bf16[128,1,4096]{2,0,1:T(8,128)(2,1)S(1)}, bf16[128,1,4096]{2,0,1:T(8,128)(2,1)}, u32[]{:S(2)}) copy-start(bf16[128,1,4096]{2,0,1:T(8,128)(2,1)} %param.6) | copy-start | bytes 3145732
  154.5 5.9 %copy-start.1 = (bf16[128,1,4096]{2,0,1:T(8,128)(2,1)S(1)}, bf16[128,1,4096]{2,0,1:T(8,128)(2,1)}, u32[]{:S(2)}) copy-start(bf16[128,1,4096]{2,0,1:T(8,128)(2,1)} %param.5) | copy-start | bytes 3145732
Sparse Core Ops, SparseCore 0:
  104.5 46.1 all-gather.2
  159.3 41.9 reduce-scatter.1

commit v2 on v1

--- a/solution.py
+++ b/solution.py
@@ -31,19 +31,9 @@
     recv = lax.all_to_all(send, FSDP, 0, 0, tiled=True)
 
     positions = jnp.arange(blocks_all, dtype=jnp.int32)
-    true_block = owner_map[member]
-    signs = (1 - 2 * sketch_seeds).astype(jnp.float32)
-    own_signs = lax.dynamic_slice_in_dim(signs, true_block * 128, 128, 0)
-    digest_row = 8.0 * jnp.einsum(
-        "k,pkc->pc", own_signs.astype(jnp.bfloat16), weights, preferred_element_type=jnp.float32
-    )
-    digest_send = digest_row.reshape(2, n_f, narrow).transpose(1, 0, 2)
-    digest_recv = lax.all_to_all(digest_send, FSDP, 0, 0, tiled=True)
-
     inverse = jnp.sum(
         jnp.where(owner_map[None, :] == positions[:, None], positions[None, :], 0), axis=1
     )
-    digest = digest_recv[inverse].transpose(1, 0, 2).reshape(2, blocks_all, 1, narrow)
 
     probe_rows = probes.shape[2]
     wide = probes.reshape(probe_rows, total_rows).astype(jnp.float32)
@@ -53,17 +43,34 @@
     normed_send = normed_send.reshape(n_rep, probe_rows, blocks_all * quarter)
     normed_recv = lax.all_to_all(normed_send, "rep", 0, 0, tiled=True)
 
+    signs = (1 - 2 * sketch_seeds).astype(jnp.float32).reshape(blocks_all, n_rep, quarter)
+    own_signs = lax.dynamic_index_in_dim(signs, replica, 1, keepdims=False)
+    sign_rows = jnp.eye(blocks_all, dtype=jnp.float32)[:, :, None] * own_signs[None, :, :]
+    sign_rows = sign_rows.reshape(blocks_all, blocks_all * quarter).astype(jnp.bfloat16)
+
     gathered = lax.all_gather(recv, "fs", axis=0, tiled=False)
     ordered = jnp.take(gathered, inverse, axis=1).transpose(1, 0, 2, 3)
     ordered = ordered.reshape(blocks_all * quarter, 2 * rank_width)
 
-    lhs = normed_recv.reshape(n_rep * probe_rows, blocks_all * quarter)
+    lhs = jnp.concatenate(
+        [normed_recv.reshape(n_rep * probe_rows, blocks_all * quarter), sign_rows], axis=0
+    )
     partial = jnp.dot(lhs, ordered, preferred_element_type=jnp.float32)
-    partial = partial.reshape(n_rep, probe_rows, 2 * rank_width)
-    summed = lax.psum_scatter(partial, "rep", scatter_dimension=0, tiled=True)
-    gate_out = summed[0, :, :rank_width]
-    up_out = summed[0, :, rank_width:]
-    hidden = (jax.nn.silu(gate_out) * up_out).astype(jnp.bfloat16)
+    hidden_part = partial[: n_rep * probe_rows].reshape(n_rep, probe_rows * 2 * rank_width)
+    digest_part = partial[n_rep * probe_rows :].reshape(blocks_all, 2, n_fs, narrow)
+    digest_part = lax.dynamic_index_in_dim(digest_part, sub, 2, keepdims=False)
+    digest_part = jnp.broadcast_to(digest_part.reshape(1, -1), (n_rep, blocks_all * 2 * narrow))
+    lanes = 128
+    packed = jnp.concatenate([hidden_part, digest_part], axis=1).reshape(n_rep, -1, lanes)
+    pieces = lax.all_to_all(packed, "rep", 0, 0, tiled=True)
+    summed = pieces[0]
+    for other in range(1, n_rep):
+        summed = summed + pieces[other]
+    summed = summed.reshape(-1)
+    hidden_sum = summed[: probe_rows * 2 * rank_width].reshape(probe_rows, 2, rank_width)
+    digest_sum = summed[probe_rows * 2 * rank_width :].reshape(blocks_all, 2, narrow)
+    digest = 8.0 * digest_sum.transpose(1, 0, 2).reshape(2, blocks_all, 1, narrow)
+    hidden = (jax.nn.silu(hidden_sum[:, 0]) * hidden_sum[:, 1]).astype(jnp.bfloat16)
     return (digest, hidden.reshape(1, 1, probe_rows, 1, rank_width))
 
 

time: 220 us -> 187 us (0.85)
  the two profiles are of different devices: /device:TPU:2 before, /device:TPU:32 now
where the time goes in v2:
time: 187 us
  blocking collectives  114 us (61%)
  waiting for transfers between devices  30.9 us (17%)
  local copies, waits for them, and re-layouts  16.6 us (9%)
  between operations  14.2 us (8%)
  other arithmetic  5.01 us (3%)
  starting transfers between devices  4.46 us (2%)
    all_to_all x1, blocking collectives, on_device(): recv = lax.all_to_all(send, FSDP, 0, 0, tiled=True)  93.3 us
    all_to_all x1, waiting for transfers between devices, on_device(): normed_recv = lax.all_to_all(normed_send, 'rep', 0, 0, tiled=True)  21.2 us
    all_to_all x1, blocking collectives, on_device(): pieces = lax.all_to_all(packed, 'rep', 0, 0, tiled=True)  20.7 us
    all_gather x1, waiting for transfers between devices, on_device(): gathered = lax.all_gather(recv, 'fs', axis=0, tiled=False)  9.7 us
    unnamed x10, local copies, waits for them, and re-layouts  5.96 us
    all_to_all x1, starting transfers between devices, on_device(): normed_recv = lax.all_to_all(normed_send, 'rep', 0, 0, tiled=True)  4.42 us
  transfers between devices with their start and end apart: 2, of which 2 were waited for; matrix products, arithmetic and copies ran while one was open for 6% of the time, Pallas kernels for 0%

profile of v2, /device:TPU:32, one launch (start us, length us, event | category | flops | bytes accessed | tf_op | source)
XLA Modules:
  0.0 186.6 jit_solution(6986113157662719660)
XLA Ops:
  7.2 1.1 fusion.5
  8.3 0.5 copy.30
  8.8 0.3 reshape.155
  9.2 93.3 %all_to_all.15 = bf16[64,8,512]{2,1,0:T(8,128)(2,1)} all-to-all(bf16[64,8,512]{2,1,0:T(8,128)(2,1)S(1)} %reshape.155), channel_id=1, replica_groups=mesh['ft'=16,'fs'=4,'rep'=4,'dp'=4] {'ft','fs'}, dimensions={0} | all-to-all | bytes 1048576 | tf_op jit(solution)/shard_map/all_to_all | solution.py:31
  102.5 3.2 %copy.26 = bf16[1,1,128,8192]{2,3,1,0:T(8,128)(2,1)S(1)} copy(bf16[1,1,128,8192]{3,2,1,0:T(8,128)(2,1)} %param.9) | data formatting | bytes 4194304 | tf_op args[4]
  105.7 1.1 multiply_reduce_fusion
  106.8 0.6 fusion.4
  107.4 1.7 copy.27
  109.1 4.4 %all-to-all-start = ((bf16[4,128,2048]{1,2,0:T(8,128)(2,1)}), bf16[4,128,2048]{1,2,0:T(8,128)(2,1)S(1)}, u32[]{:S(2)}, u32[]{:S(2)}) async-start(bf16[4,128,2048]{1,2,0:T(8,128)(2,1)} %bitcast.45), calls=%async_computation | async-start | bytes 4194304 | tf_op jit(solution)/shard_map/all_to_all | solution.py:44
  114.0 1.1 copy.29
  115.2 1.1 multiply_convert_fusion
  116.3 21.2 %all-to-all-done = bf16[4,128,2048]{1,2,0:T(8,128)(2,1)S(1)} async-done(((bf16[4,128,2048]{1,2,0:T(8,128)(2,1)}), bf16[4,128,2048]{1,2,0:T(8,128)(2,1)S(1)}, u32[]{:S(2)}, u32[]{:S(2)}) %all-to-all-start) | async-done | bytes 2097184 | tf_op jit(solution)/shard_map/all_to_all | solution.py:44
  137.5 2.7 %copy.28 = bf16[4,128,2048]{2,1,0:T(8,128)(2,1)} copy(bf16[4,128,2048]{1,2,0:T(8,128)(2,1)S(1)} %all-to-all-done) | data formatting | bytes 4194304 | tf_op jit(solution)/shard_map/all_to_all | solution.py:44
  140.2 9.7 %all-gather.3.cloned.1.call-done = bf16[256,8,512]{2,1,0:T(8,128)(2,1)} async-done(((bf16[64,8,512]{2,1,0:T(8,128)(2,1)}), bf16[256,8,512]{2,1,0:T(8,128)(2,1)}) %all-gather.3.cloned.1.call-update) | async-done | bytes 2097168 | tf_op jit(solution)/shard_map/all_gather | solution.py:51
  149.9 2.3 %gather_fusion = bf16[64,4,8,512]{3,2,1,0:T(8,128)(2,1)S(1)} fusion(bf16[4,64,8,512]{3,2,1,0:T(8,128)(2,1)} %bitcast.48, s32[1024]{0:T(1024)S(1)} %pad_clamp_fusion), kind=kCustom, calls=%fused_computation | custom fusion | bytes 4194560 | tf_op jit(solution)/shard_map/jit(_take)/gather | solution.py:52
  152.2 0.3 broadcast_select_fusion
  152.5 1.3 copy-done
  153.8 1.4 fusion
  155.3 0.7 reshape.157
  156.5 0.4 maximum_bitcast_fusion
  157.0 20.7 %all_to_all.16 = f32[4,576,128]{2,1,0:T(8,128)S(1)} all-to-all(f32[4,576,128]{2,1,0:T(8,128)S(1)} %bitcast.46), channel_id=1, replica_groups=mesh['ft'=16,'fs'=4,'rep'=4,'dp'=4] {'rep'}, dimensions={0} | all-to-all | bytes 2359296 | tf_op jit(solution)/shard_map/all_to_all | solution.py:65
  178.0 0.3 fusion.7
  178.3 0.6 copy.32
  179.0 0.7 copy.31
  (30 shorter events, 1.6 us)
Async XLA Ops:
  7.2 142.7 %all-gather.3.cloned.1.call-start = ((), (), s32[]{:S(2)}) async-start(), calls=%async_computation.3 | async-start | bytes 2621440 | tf_op jit(solution)/shard_map/all_gather | solution.py:51
  109.1 4.4 %copy-start.1 = (s32[8192]{0:T(1024)S(1)}, s32[8192]{0:T(1024)}, u32[]{:S(2)}) copy-start(s32[8192]{0:T(1024)} %param.8) | copy-start | bytes 98308
  109.1 28.4 %all-to-all-start = ((bf16[4,128,2048]{1,2,0:T(8,128)(2,1)}), bf16[4,128,2048]{1,2,0:T(8,128)(2,1)S(1)}, u32[]{:S(2)}, u32[]{:S(2)}) async-start(bf16[4,128,2048]{1,2,0:T(8,128)(2,1)} %bitcast.45), calls=%async_computation | async-start | bytes 4194304 | tf_op jit(solution)/shard_map/all_to_all | solution.py:44
  113.5 1.5 copy-start.2
  152.2 1.6 copy-start
Sparse Core Ops, SparseCore 0:
  102.6 47.2 all-gather.2

commit v3 on v2

--- a/solution.py
+++ b/solution.py
@@ -27,8 +27,7 @@
 
     mine = lax.dynamic_slice_in_dim(weights, replica * quarter, quarter, 1)
     send = mine.reshape(2, n_fs, piece, n_ft, rank_width).transpose(3, 1, 2, 0, 4)
-    send = send.reshape(n_f, piece, 2 * rank_width)
-    recv = lax.all_to_all(send, FSDP, 0, 0, tiled=True)
+    send = send.reshape(n_ft, n_fs * piece, 2 * rank_width)
 
     positions = jnp.arange(blocks_all, dtype=jnp.int32)
     inverse = jnp.sum(
@@ -41,15 +40,28 @@
     normed = (wide / jnp.sqrt(meansq + 1e-05)).astype(jnp.bfloat16)
     normed_send = normed.reshape(probe_rows, blocks_all, n_rep, quarter).transpose(2, 0, 1, 3)
     normed_send = normed_send.reshape(n_rep, probe_rows, blocks_all * quarter)
-    normed_recv = lax.all_to_all(normed_send, "rep", 0, 0, tiled=True)
 
     signs = (1 - 2 * sketch_seeds).astype(jnp.float32).reshape(blocks_all, n_rep, quarter)
     own_signs = lax.dynamic_index_in_dim(signs, replica, 1, keepdims=False)
     sign_rows = jnp.eye(blocks_all, dtype=jnp.float32)[:, :, None] * own_signs[None, :, :]
     sign_rows = sign_rows.reshape(blocks_all, blocks_all * quarter).astype(jnp.bfloat16)
 
-    gathered = lax.all_gather(recv, "fs", axis=0, tiled=False)
-    ordered = jnp.take(gathered, inverse, axis=1).transpose(1, 0, 2, 3)
+    send, normed_send = lax.optimization_barrier((send, normed_send))
+    normed_recv = lax.all_to_all(normed_send, "rep", 0, 0, tiled=True)
+    recv = lax.all_to_all(send, "ft", 0, 0, tiled=True)
+    shared = [recv]
+    for shift in range(1, n_fs):
+        pairs = [(i, i ^ shift) for i in range(n_fs)]
+        shared.append(lax.ppermute(recv, "fs", pairs))
+    gathered = jnp.stack([shared[k] for k in range(n_fs)])
+    source_of = sub ^ jnp.arange(n_fs, dtype=jnp.int32)
+    gathered = gathered.reshape(n_fs, n_ft, quarter, 2 * rank_width)
+    block_src = (jnp.arange(n_ft, dtype=jnp.int32)[None, :] * n_fs + source_of[:, None]).reshape(-1)
+    gathered = gathered.reshape(n_fs * n_ft, quarter, 2 * rank_width)
+    where_block = jnp.sum(
+        jnp.where(block_src[None, :] == inverse[:, None], positions[None, :], 0), axis=1
+    )
+    ordered = jnp.take(gathered, where_block, axis=0)
     ordered = ordered.reshape(blocks_all * quarter, 2 * rank_width)
 
     lhs = jnp.concatenate(

time: 187 us -> 164 us (0.88)
  the two profiles are of different devices: /device:TPU:32 before, /device:TPU:64 now
where the time goes in v3:
time: 164 us
  waiting for transfers between devices  76.1 us (46%)
  starting transfers between devices  41.5 us (25%)
  blocking collectives  18.9 us (12%)
  local copies, waits for them, and re-layouts  16.4 us (10%)
  other arithmetic  8.68 us (5%)
    all_to_all x1, waiting for transfers between devices, on_device(): recv = lax.all_to_all(send, 'ft', 0, 0, tiled=True)  57.6 us
    all_to_all x1, starting transfers between devices, on_device(): recv = lax.all_to_all(send, 'ft', 0, 0, tiled=True)  28 us
    all_to_all x1, blocking collectives, on_device(): pieces = lax.all_to_all(packed, 'rep', 0, 0, tiled=True)  18.9 us
    all_to_all x1, waiting for transfers between devices, on_device(): normed_recv = lax.all_to_all(normed_send, 'rep', 0, 0, tiled=True)  14 us
    ppermute x3, starting transfers between devices, on_device(): shared.append(lax.ppermute(recv, 'fs', pairs))  9.22 us
    unnamed x10, local copies, waits for them, and re-layouts  4.93 us
    ppermute x3, waiting for transfers between devices, on_device(): shared.append(lax.ppermute(recv, 'fs', pairs))  4.48 us
    all_to_all x1, starting transfers between devices, on_device(): normed_recv = lax.all_to_all(normed_send, 'rep', 0, 0, tiled=True)  4.29 us
  transfers between devices with their start and end apart: 5, of which 3 were waited for; matrix products, arithmetic and copies ran while one was open for 4% of the time, Pallas kernels for 0%

profile of v3, /device:TPU:64, one launch (start us, length us, event | category | flops | bytes accessed | tf_op | source)
XLA Modules:
  0.0 163.8 jit_solution(8189422755970869730)
XLA Ops:
  0.6 1.1 fusion.5
  2.3 1.1 reshape.179
  3.4 3.2 %copy.20 = bf16[1,1,128,8192]{2,3,1,0:T(8,128)(2,1)S(1)} copy(bf16[1,1,128,8192]{3,2,1,0:T(8,128)(2,1)} %param.9) | data formatting | bytes 4194304 | tf_op args[4]
  6.6 1.1 multiply_reduce_fusion
  8.3 1.8 %copy.21 = bf16[4,128,64,32]{1,3,2,0:T(8,128)(2,1)} copy(bf16[4,128,64,32]{1,3,0,2:T(8,128)(2,1)S(1)} %fusion.4) | data formatting | bytes 4194304 | tf_op jit(solution)/shard_map/transpose | solution.py:41
  10.1 28.0 %all-to-all-start.1 = ((bf16[16,32,512]{2,1,0:T(8,128)(2,1)}), bf16[16,32,512]{2,1,0:T(8,128)(2,1)}, u32[]{:S(2)}, u32[]{:S(2)}) async-start(bf16[16,32,512]{2,1,0:T(8,128)(2,1)} %reshape.179), calls=%async_computation.1 | async-start | bytes 1048576 | tf_op jit(solution)/shard_map/all_to_all | solution.py:51
  38.3 57.6 %all-to-all-done.1 = bf16[16,32,512]{2,1,0:T(8,128)(2,1)} async-done(((bf16[16,32,512]{2,1,0:T(8,128)(2,1)}), bf16[16,32,512]{2,1,0:T(8,128)(2,1)}, u32[]{:S(2)}, u32[]{:S(2)}) %all-to-all-start.1) | async-done | bytes 524320 | tf_op jit(solution)/shard_map/all_to_all | solution.py:51
  95.9 4.3 %all-to-all-start = ((bf16[4,128,2048]{1,2,0:T(8,128)(2,1)}), bf16[4,128,2048]{1,2,0:T(8,128)(2,1)S(1)}, u32[]{:S(2)}, u32[]{:S(2)}) async-start(bf16[4,128,2048]{1,2,0:T(8,128)(2,1)} %bitcast.5), calls=%async_computation | async-start | bytes 4194304 | tf_op jit(solution)/shard_map/all_to_all | solution.py:50
  100.6 1.9 %collective-permute-start.1 = (bf16[16,32,512]{2,1,0:T(8,128)(2,1)}, bf16[16,32,512]{2,1,0:T(8,128)(2,1)}, u32[]{:S(2)}, u32[]{:S(2)}) collective-permute-start(bf16[16,32,512]{2,1,0:T(8,128)(2,1)} %all-to-all-done.1), channel_id=1, source_target_pairs={{0,32},{16,48},{32,0},{48,16},{1,33},{17,49},{33,1},{49,17},{2,34}... | collective-permute-start | bytes 1572872 | tf_op jit(solution)/shard_map/ppermute | solution.py:55
  102.5 4.9 %collective-permute-start.2 = (bf16[16,32,512]{2,1,0:T(8,128)(2,1)}, bf16[16,32,512]{2,1,0:T(8,128)(2,1)}, u32[]{:S(2)}, u32[]{:S(2)}) collective-permute-start(bf16[16,32,512]{2,1,0:T(8,128)(2,1)} %all-to-all-done.1), channel_id=1, source_target_pairs={{0,48},{16,32},{32,16},{48,0},{1,49},{17,33},{33,17},{49,1},{2,50}... | collective-permute-start | bytes 1572872 | tf_op jit(solution)/shard_map/ppermute | solution.py:55
  107.4 2.4 %collective-permute-start = (bf16[16,32,512]{2,1,0:T(8,128)(2,1)}, bf16[16,32,512]{2,1,0:T(8,128)(2,1)}, u32[]{:S(2)}, u32[]{:S(2)}) collective-permute-start(bf16[16,32,512]{2,1,0:T(8,128)(2,1)} %all-to-all-done.1), channel_id=1, source_target_pairs={{0,16},{16,0},{32,48},{48,32},{1,17},{17,1},{33,49},{49,33},{2,18}... | collective-permute-start | bytes 1572872 | tf_op jit(solution)/shard_map/ppermute | solution.py:55
  110.4 1.1 copy.23
  111.5 1.1 multiply_convert_fusion
  112.6 14.0 %all-to-all-done = bf16[4,128,2048]{1,2,0:T(8,128)(2,1)S(1)} async-done(((bf16[4,128,2048]{1,2,0:T(8,128)(2,1)}), bf16[4,128,2048]{1,2,0:T(8,128)(2,1)S(1)}, u32[]{:S(2)}, u32[]{:S(2)}) %all-to-all-start) | async-done | bytes 2097184 | tf_op jit(solution)/shard_map/all_to_all | solution.py:50
  126.6 2.7 %copy.22 = bf16[4,128,2048]{2,1,0:T(8,128)(2,1)} copy(bf16[4,128,2048]{1,2,0:T(8,128)(2,1)S(1)} %all-to-all-done) | data formatting | bytes 4194304 | tf_op jit(solution)/shard_map/all_to_all | solution.py:50
  129.3 4.5 %collective-permute-done = bf16[16,32,512]{2,1,0:T(8,128)(2,1)} collective-permute-done((bf16[16,32,512]{2,1,0:T(8,128)(2,1)}, bf16[16,32,512]{2,1,0:T(8,128)(2,1)}, u32[]{:S(2)}, u32[]{:S(2)}) %collective-permute-start) | collective-permute-done | bytes 524320 | tf_op jit(solution)/shard_map/ppermute | solution.py:55
  133.8 1.8 %pad_maximum_fusion = bf16[4,16,32,512]{3,2,1,0:T(8,128)(2,1)S(1)} fusion(bf16[1,16,32,512]{3,2,1,0:T(8,128)(2,1)} %bitcast.11, bf16[1,16,32,512]{3,2,1,0:T(8,128)(2,1)} %bitcast.10, bf16[1,16,32,512]{3,2,1,0:T(8,128)(2,1)} %bitcast.9, bf16[1,16,32,512]{3,2,1,0:T(8,128)(2,1)} %bitcast.8), kind=kLoop, calls=%fused_computation.9 | loop fusion | flops 3145728 | bytes 4194304 | tf_op jit(solution)/shard_map/stack | solution.py:56
  135.5 2.0 %gather_fusion = bf16[64,32,512]{2,1,0:T(8,128)(2,1)} fusion(bf16[64,32,512]{2,1,0:T(8,128)(2,1)S(1)} %bitcast.50, s32[1024]{0:T(1024)S(1)} %pad_clamp_fusion), kind=kCustom, calls=%fused_computation | custom fusion | bytes 4194560 | tf_op jit(solution)/shard_map/jit(_take)/gather | solution.py:64
  137.5 1.9 %bitcast_select_fusion = bf16[2048,512]{1,0:T(8,128)(2,1)S(1)} fusion(bf16[64,32,512]{2,1,0:T(8,128)(2,1)} %gather_fusion, pred[2048]{0:T(1024)(128)(4,1)S(1)} %broadcast_in_dim.53), kind=kLoop, calls=%fused_computation.10 | loop fusion | flops 1048576 | bytes 4196352 | tf_op jit(solution)/shard_map/jit(_take)/select_n | solution.py:64
  139.7 1.4 fusion
  141.2 0.7 reshape.184
  142.9 18.9 %all_to_all.15 = f32[4,576,128]{2,1,0:T(8,128)S(1)} all-to-all(f32[4,576,128]{2,1,0:T(8,128)S(1)} %bitcast.51), channel_id=1, replica_groups=mesh['ft'=16,'fs'=4,'rep'=4,'dp'=4] {'rep'}, dimensions={0} | all-to-all | bytes 2359296 | tf_op jit(solution)/shard_map/all_to_all | solution.py:77
  162.4 0.6 copy.25
  163.1 0.7 copy.24
  (42 shorter events, 4.2 us)
Async XLA Ops:
  10.1 85.8 %all-to-all-start.1 = ((bf16[16,32,512]{2,1,0:T(8,128)(2,1)}), bf16[16,32,512]{2,1,0:T(8,128)(2,1)}, u32[]{:S(2)}, u32[]{:S(2)}) async-start(bf16[16,32,512]{2,1,0:T(8,128)(2,1)} %reshape.179), calls=%async_computation.1 | async-start | bytes 1048576 | tf_op jit(solution)/shard_map/all_to_all | solution.py:51
  38.3 61.9 %copy-start.2 = (s32[64]{0:T(128)S(1)}, s32[64]{0:T(128)}, u32[]{:S(2)}) copy-start(s32[64]{0:T(128)} %param.7) | copy-start | bytes 772
  38.3 62.3 %copy-start.1 = (s32[8192]{0:T(1024)S(1)}, s32[8192]{0:T(1024)}, u32[]{:S(2)}) copy-start(s32[8192]{0:T(1024)} %param.8) | copy-start | bytes 98308
  95.9 30.7 %all-to-all-start = ((bf16[4,128,2048]{1,2,0:T(8,128)(2,1)}), bf16[4,128,2048]{1,2,0:T(8,128)(2,1)S(1)}, u32[]{:S(2)}, u32[]{:S(2)}) async-start(bf16[4,128,2048]{1,2,0:T(8,128)(2,1)} %bitcast.5), calls=%async_computation | async-start | bytes 4194304 | tf_op jit(solution)/shard_map/all_to_all | solution.py:50
  100.6 28.7 %collective-permute-start.1 = (bf16[16,32,512]{2,1,0:T(8,128)(2,1)}, bf16[16,32,512]{2,1,0:T(8,128)(2,1)}, u32[]{:S(2)}, u32[]{:S(2)}) collective-permute-start(bf16[16,32,512]{2,1,0:T(8,128)(2,1)} %all-to-all-done.1), channel_id=1, source_target_pairs={{0,32},{16,48},{32,0},{48,16},{1,33},{17,49},{33,1},{49,17},{2,34}... | collective-permute-start | bytes 1572872 | tf_op jit(solution)/shard_map/ppermute | solution.py:55
  102.5 26.8 %collective-permute-start.2 = (bf16[16,32,512]{2,1,0:T(8,128)(2,1)}, bf16[16,32,512]{2,1,0:T(8,128)(2,1)}, u32[]{:S(2)}, u32[]{:S(2)}) collective-permute-start(bf16[16,32,512]{2,1,0:T(8,128)(2,1)} %all-to-all-done.1), channel_id=1, source_target_pairs={{0,48},{16,32},{32,16},{48,0},{1,49},{17,33},{33,17},{49,1},{2,50}... | collective-permute-start | bytes 1572872 | tf_op jit(solution)/shard_map/ppermute | solution.py:55
  107.4 26.3 %collective-permute-start = (bf16[16,32,512]{2,1,0:T(8,128)(2,1)}, bf16[16,32,512]{2,1,0:T(8,128)(2,1)}, u32[]{:S(2)}, u32[]{:S(2)}) collective-permute-start(bf16[16,32,512]{2,1,0:T(8,128)(2,1)} %all-to-all-done.1), channel_id=1, source_target_pairs={{0,16},{16,0},{32,48},{48,32},{1,17},{17,1},{33,49},{49,33},{2,18}... | collective-permute-start | bytes 1572872 | tf_op jit(solution)/shard_map/ppermute | solution.py:55
  137.5 2.2 %copy-start = (bf16[4,128,2048]{2,1,0:T(8,128)(2,1)S(1)}, bf16[4,128,2048]{2,1,0:T(8,128)(2,1)}, u32[]{:S(2)}) copy-start(bf16[4,128,2048]{2,1,0:T(8,128)(2,1)} %copy.22) | copy-start | bytes 6291460

commit v4 on v2

--- a/solution.py
+++ b/solution.py
@@ -26,9 +26,8 @@
     weights = jnp.stack([trainer_gate.reshape(rows, width), trainer_up.reshape(rows, width)])
 
     mine = lax.dynamic_slice_in_dim(weights, replica * quarter, quarter, 1)
-    send = mine.reshape(2, n_fs, piece, n_ft, rank_width).transpose(3, 1, 2, 0, 4)
-    send = send.reshape(n_f, piece, 2 * rank_width)
-    recv = lax.all_to_all(send, FSDP, 0, 0, tiled=True)
+    send = mine.reshape(2, n_fs, piece, n_ft, rank_width).transpose(0, 3, 1, 2, 4)
+    send = send.reshape(2, n_ft, n_fs * piece, rank_width)
 
     positions = jnp.arange(blocks_all, dtype=jnp.int32)
     inverse = jnp.sum(
@@ -41,28 +40,53 @@
     normed = (wide / jnp.sqrt(meansq + 1e-05)).astype(jnp.bfloat16)
     normed_send = normed.reshape(probe_rows, blocks_all, n_rep, quarter).transpose(2, 0, 1, 3)
     normed_send = normed_send.reshape(n_rep, probe_rows, blocks_all * quarter)
-    normed_recv = lax.all_to_all(normed_send, "rep", 0, 0, tiled=True)
 
     signs = (1 - 2 * sketch_seeds).astype(jnp.float32).reshape(blocks_all, n_rep, quarter)
     own_signs = lax.dynamic_index_in_dim(signs, replica, 1, keepdims=False)
     sign_rows = jnp.eye(blocks_all, dtype=jnp.float32)[:, :, None] * own_signs[None, :, :]
     sign_rows = sign_rows.reshape(blocks_all, blocks_all * quarter).astype(jnp.bfloat16)
 
-    gathered = lax.all_gather(recv, "fs", axis=0, tiled=False)
-    ordered = jnp.take(gathered, inverse, axis=1).transpose(1, 0, 2, 3)
-    ordered = ordered.reshape(blocks_all * quarter, 2 * rank_width)
+    chunks = [
+        lax.dynamic_index_in_dim(normed_send, (replica + k) % n_rep, 0, keepdims=False)
+        for k in range(n_rep)
+    ]
+    chunks = list(lax.optimization_barrier((send, *chunks)))
+    send, chunks = chunks[0], chunks[1:]
+    normed_got = [chunks[0]]
+    for k in range(1, n_rep):
+        pairs = [(i, (i + k) % n_rep) for i in range(n_rep)]
+        normed_got.append(lax.ppermute(chunks[k], "rep", pairs))
+    source_of = sub ^ jnp.arange(n_fs, dtype=jnp.int32)
+    block_src = (jnp.arange(n_ft, dtype=jnp.int32)[None, :] * n_fs + source_of[:, None]).reshape(-1)
+    where_block = jnp.sum(
+        jnp.where(block_src[None, :] == inverse[:, None], positions[None, :], 0), axis=1
+    )
+    lhs = jnp.concatenate([*normed_got, sign_rows], axis=0)
 
-    lhs = jnp.concatenate(
-        [normed_recv.reshape(n_rep * probe_rows, blocks_all * quarter), sign_rows], axis=0
-    )
-    partial = jnp.dot(lhs, ordered, preferred_element_type=jnp.float32)
+    partials = []
+    for proj in range(2):
+        recv = lax.all_to_all(send[proj], "ft", 0, 0, tiled=True)
+        shared = [recv]
+        for shift in range(1, n_fs):
+            pairs = [(i, i ^ shift) for i in range(n_fs)]
+            shared.append(lax.ppermute(recv, "fs", pairs))
+        gathered = jnp.stack(shared).reshape(n_fs * n_ft, quarter, rank_width)
+        ordered = jnp.take(gathered, where_block, axis=0)
+        ordered = ordered.reshape(blocks_all * quarter, rank_width)
+        partials.append(jnp.dot(lhs, ordered, preferred_element_type=jnp.float32))
+    partial = jnp.concatenate(partials, axis=1)
     hidden_part = partial[: n_rep * probe_rows].reshape(n_rep, probe_rows * 2 * rank_width)
     digest_part = partial[n_rep * probe_rows :].reshape(blocks_all, 2, n_fs, narrow)
     digest_part = lax.dynamic_index_in_dim(digest_part, sub, 2, keepdims=False)
     digest_part = jnp.broadcast_to(digest_part.reshape(1, -1), (n_rep, blocks_all * 2 * narrow))
     lanes = 128
     packed = jnp.concatenate([hidden_part, digest_part], axis=1).reshape(n_rep, -1, lanes)
-    pieces = lax.all_to_all(packed, "rep", 0, 0, tiled=True)
+    back = [packed[0]]
+    for k in range(1, n_rep):
+        pairs = [(i, (i - k) % n_rep) for i in range(n_rep)]
+        back.append(lax.ppermute(packed[k], "rep", pairs))
+    slot_of = (jnp.arange(n_rep, dtype=jnp.int32) - replica) % n_rep
+    pieces = jnp.take(jnp.stack(back), slot_of, axis=0)
     summed = pieces[0]
     for other in range(1, n_rep):
         summed = summed + pieces[other]

time: 187 us -> 167 us (0.89)
  the two profiles are of different devices: /device:TPU:32 before, /device:TPU:66 now
where the time goes in v4:
time: 167 us; the launch traced here: 166 us
  starting transfers between devices  74.6 us (45%)
  waiting for transfers between devices  65.1 us (39%)
  local copies, waits for them, and re-layouts  16.8 us (10%)
  other arithmetic  7.15 us (4%)
  matrix products  1.75 us (1%)
    all_to_all x2, waiting for transfers between devices, on_device(): recv = lax.all_to_all(send[proj], 'ft', 0, 0, tiled=True)  51.7 us
    all_to_all x2, starting transfers between devices, on_device(): recv = lax.all_to_all(send[proj], 'ft', 0, 0, tiled=True)  35.3 us
    ppermute x6, starting transfers between devices, on_device(): shared.append(lax.ppermute(recv, 'fs', pairs))  18.4 us
    ppermute x3, starting transfers between devices, on_device(): back.append(lax.ppermute(packed[k], 'rep', pairs))  10.5 us
    ppermute x3, starting transfers between devices, on_device(): normed_got.append(lax.ppermute(chunks[k], 'rep', pairs))  10.5 us
    unnamed x14, local copies, waits for them, and re-layouts  9.63 us
    ppermute x3, waiting for transfers between devices, on_device(): back.append(lax.ppermute(packed[k], 'rep', pairs))  9.39 us
    ppermute x6, waiting for transfers between devices, on_device(): shared.append(lax.ppermute(recv, 'fs', pairs))  4.05 us
  transfers between devices with their start and end apart: 14, of which 7 were waited for; matrix products, arithmetic and copies ran while one was open for 4% of the time, Pallas kernels for 0%

profile of v4, /device:TPU:66, one launch (start us, length us, event | category | flops | bytes accessed | tf_op | source)
XLA Modules:
  0.0 166.5 jit_solution(12792767021362137530)
XLA Ops:
  2.0 3.2 %copy.17 = bf16[1,1,128,8192]{2,3,1,0:T(8,128)(2,1)S(1)} copy(bf16[1,1,128,8192]{3,2,1,0:T(8,128)(2,1)} %param.11) | data formatting | bytes 4194304 | tf_op args[4]
  9.4 28.0 %all-to-all-start.1 = ((bf16[16,32,256]{2,1,0:T(8,128)(2,1)}), bf16[16,32,256]{2,1,0:T(8,128)(2,1)S(1)}, u32[]{:S(2)}, u32[]{:S(2)}) async-start(bf16[16,32,256]{2,1,0:T(8,128)(2,1)} %get-tuple-element.27), calls=%async_computation.1 | async-start | bytes 524288 | tf_op jit(solution)/shard_map/all_to_all | solution.py:68
  37.4 3.4 %collective-permute-start = (bf16[128,2048]{0,1:T(8,128)(2,1)}, bf16[128,2048]{0,1:T(8,128)(2,1)S(1)}, u32[]{:S(2)}, u32[]{:S(2)}) collective-permute-start(bf16[128,2048]{0,1:T(8,128)(2,1)} %get-tuple-element.9), channel_id=1, source_target_pairs={{0,4},{4,8},{8,12},{12,0},{1,5},{5,9},{9,13},{13,1},{2,6},{6,10},{... | collective-permute-start | bytes 1572872 | tf_op jit(solution)/shard_map/ppermute | solution.py:58
  40.8 3.0 %collective-permute-start.1 = (bf16[128,2048]{0,1:T(8,128)(2,1)}, bf16[128,2048]{0,1:T(8,128)(2,1)S(1)}, u32[]{:S(2)}, u32[]{:S(2)}) collective-permute-start(bf16[128,2048]{0,1:T(8,128)(2,1)} %get-tuple-element.10), channel_id=1, source_target_pairs={{0,8},{4,12},{8,0},{12,4},{1,9},{5,13},{9,1},{13,5},{2,10},{6,14},... | collective-permute-start | bytes 1572872 | tf_op jit(solution)/shard_map/ppermute | solution.py:58
  43.8 4.1 %collective-permute-start.2 = (bf16[128,2048]{0,1:T(8,128)(2,1)}, bf16[128,2048]{0,1:T(8,128)(2,1)S(1)}, u32[]{:S(2)}, u32[]{:S(2)}) collective-permute-start(bf16[128,2048]{0,1:T(8,128)(2,1)} %get-tuple-element.11), channel_id=1, source_target_pairs={{0,12},{4,0},{8,4},{12,8},{1,13},{5,1},{9,5},{13,9},{2,14},{6,2},{... | collective-permute-start | bytes 1572872 | tf_op jit(solution)/shard_map/ppermute | solution.py:58
  47.9 27.2 %all-to-all-done.1 = bf16[16,32,256]{2,1,0:T(8,128)(2,1)S(1)} async-done(((bf16[16,32,256]{2,1,0:T(8,128)(2,1)}), bf16[16,32,256]{2,1,0:T(8,128)(2,1)S(1)}, u32[]{:S(2)}, u32[]{:S(2)}) %all-to-all-start.1) | async-done | bytes 262176 | tf_op jit(solution)/shard_map/all_to_all | solution.py:68
  75.1 7.2 %all-to-all-start = ((bf16[16,32,256]{2,1,0:T(8,128)(2,1)}), bf16[16,32,256]{2,1,0:T(8,128)(2,1)S(1)}, u32[]{:S(2)}, u32[]{:S(2)}) async-start(bf16[16,32,256]{2,1,0:T(8,128)(2,1)} %get-tuple-element.28), calls=%async_computation | async-start | bytes 524288 | tf_op jit(solution)/shard_map/all_to_all | solution.py:68
  84.1 3.9 %collective-permute-start.8 = (bf16[16,32,256]{2,1,0:T(8,128)(2,1)S(1)}, bf16[16,32,256]{2,1,0:T(8,128)(2,1)S(1)}, u32[]{:S(2)}, u32[]{:S(2)}) collective-permute-start(bf16[16,32,256]{2,1,0:T(8,128)(2,1)S(1)} %all-to-all-done.1), channel_id=1, source_target_pairs={{0,48},{16,32},{32,16},{48,0},{1,49},{17,33},{33,17},{49,1},{2,50}... | collective-permute-start | bytes 786440 | tf_op jit(solution)/shard_map/ppermute | solution.py:72
  88.9 2.9 %collective-permute-start.7 = (bf16[16,32,256]{2,1,0:T(8,128)(2,1)S(1)}, bf16[16,32,256]{2,1,0:T(8,128)(2,1)S(1)}, u32[]{:S(2)}, u32[]{:S(2)}) collective-permute-start(bf16[16,32,256]{2,1,0:T(8,128)(2,1)S(1)} %all-to-all-done.1), channel_id=1, source_target_pairs={{0,32},{16,48},{32,0},{48,16},{1,33},{17,49},{33,1},{49,17},{2,34}... | collective-permute-start | bytes 786440 | tf_op jit(solution)/shard_map/ppermute | solution.py:72
  91.8 2.4 %collective-permute-start.6 = (bf16[16,32,256]{2,1,0:T(8,128)(2,1)S(1)}, bf16[16,32,256]{2,1,0:T(8,128)(2,1)S(1)}, u32[]{:S(2)}, u32[]{:S(2)}) collective-permute-start(bf16[16,32,256]{2,1,0:T(8,128)(2,1)S(1)} %all-to-all-done.1), channel_id=1, source_target_pairs={{0,16},{16,0},{32,48},{48,32},{1,17},{17,1},{33,49},{49,33},{2,18}... | collective-permute-start | bytes 786440 | tf_op jit(solution)/shard_map/ppermute | solution.py:72
  95.1 24.4 %all-to-all-done = bf16[16,32,256]{2,1,0:T(8,128)(2,1)S(1)} async-done(((bf16[16,32,256]{2,1,0:T(8,128)(2,1)}), bf16[16,32,256]{2,1,0:T(8,128)(2,1)S(1)}, u32[]{:S(2)}, u32[]{:S(2)}) %all-to-all-start) | async-done | bytes 262176 | tf_op jit(solution)/shard_map/all_to_all | solution.py:68
  119.5 1.9 %collective-permute-start.5 = (bf16[16,32,256]{2,1,0:T(8,128)(2,1)S(1)}, bf16[16,32,256]{2,1,0:T(8,128)(2,1)}, u32[]{:S(2)}, u32[]{:S(2)}) collective-permute-start(bf16[16,32,256]{2,1,0:T(8,128)(2,1)S(1)} %all-to-all-done), channel_id=1, source_target_pairs={{0,48},{16,32},{32,16},{48,0},{1,49},{17,33},{33,17},{49,1},{2,50}... | collective-permute-start | bytes 786440 | tf_op jit(solution)/shard_map/ppermute | solution.py:72
  121.4 4.9 %collective-permute-start.4 = (bf16[16,32,256]{2,1,0:T(8,128)(2,1)S(1)}, bf16[16,32,256]{2,1,0:T(8,128)(2,1)}, u32[]{:S(2)}, u32[]{:S(2)}) collective-permute-start(bf16[16,32,256]{2,1,0:T(8,128)(2,1)S(1)} %all-to-all-done), channel_id=1, source_target_pairs={{0,32},{16,48},{32,0},{48,16},{1,33},{17,49},{33,1},{49,17},{2,34}... | collective-permute-start | bytes 786440 | tf_op jit(solution)/shard_map/ppermute | solution.py:72
  126.4 2.4 %collective-permute-start.3 = (bf16[16,32,256]{2,1,0:T(8,128)(2,1)S(1)}, bf16[16,32,256]{2,1,0:T(8,128)(2,1)}, u32[]{:S(2)}, u32[]{:S(2)}) collective-permute-start(bf16[16,32,256]{2,1,0:T(8,128)(2,1)S(1)} %all-to-all-done), channel_id=1, source_target_pairs={{0,16},{16,0},{32,48},{48,32},{1,17},{17,1},{33,49},{49,33},{2,18}... | collective-permute-start | bytes 786440 | tf_op jit(solution)/shard_map/ppermute | solution.py:72
  129.6 1.2 constant_dynamic-update-slice_fusion
  131.6 2.8 %collective-permute-done.4 = bf16[16,32,256]{2,1,0:T(8,128)(2,1)} collective-permute-done((bf16[16,32,256]{2,1,0:T(8,128)(2,1)S(1)}, bf16[16,32,256]{2,1,0:T(8,128)(2,1)}, u32[]{:S(2)}, u32[]{:S(2)}) %collective-permute-start.4) | collective-permute-done | bytes 262176 | tf_op jit(solution)/shard_map/ppermute | solution.py:72
  134.3 1.3 collective-permute-done.3
  135.6 1.2 pad_maximum_fusion.2
  137.7 1.5 copy-done
  143.6 3.4 %collective-permute-start.11 = (f32[576,128]{1,0:T(8,128)S(1)}, f32[576,128]{1,0:T(8,128)S(1)}, u32[]{:S(2)}, u32[]{:S(2)}) collective-permute-start(f32[576,128]{1,0:T(8,128)S(1)} %bitcast.90), channel_id=1, source_target_pairs={{0,4},{4,8},{8,12},{12,0},{1,5},{5,9},{9,13},{13,1},{2,6},{6,10},{... | collective-permute-start | bytes 884744 | tf_op jit(solution)/shard_map/ppermute | solution.py:87
  147.0 3.0 %collective-permute-start.10 = (f32[576,128]{1,0:T(8,128)S(1)}, f32[576,128]{1,0:T(8,128)S(1)}, u32[]{:S(2)}, u32[]{:S(2)}) collective-permute-start(f32[576,128]{1,0:T(8,128)S(1)} %bitcast.88), channel_id=1, source_target_pairs={{0,8},{4,12},{8,0},{12,4},{1,9},{5,13},{9,1},{13,5},{2,10},{6,14},... | collective-permute-start | bytes 884744 | tf_op jit(solution)/shard_map/ppermute | solution.py:87
  150.1 4.1 %collective-permute-start.9 = (f32[576,128]{1,0:T(8,128)S(1)}, f32[576,128]{1,0:T(8,128)S(1)}, u32[]{:S(2)}, u32[]{:S(2)}) collective-permute-start(f32[576,128]{1,0:T(8,128)S(1)} %bitcast.86), channel_id=1, source_target_pairs={{0,12},{4,0},{8,4},{12,8},{1,13},{5,1},{9,5},{13,9},{2,14},{6,2},{... | collective-permute-start | bytes 884744 | tf_op jit(solution)/shard_map/ppermute | solution.py:87
  154.6 5.8 %collective-permute-done.10 = f32[576,128]{1,0:T(8,128)S(1)} collective-permute-done((f32[576,128]{1,0:T(8,128)S(1)}, f32[576,128]{1,0:T(8,128)S(1)}, u32[]{:S(2)}, u32[]{:S(2)}) %collective-permute-start.10) | collective-permute-done | bytes 294944 | tf_op jit(solution)/shard_map/ppermute | solution.py:87
  160.3 3.2 %collective-permute-done.9 = f32[576,128]{1,0:T(8,128)S(1)} collective-permute-done((f32[576,128]{1,0:T(8,128)S(1)}, f32[576,128]{1,0:T(8,128)S(1)}, u32[]{:S(2)}, u32[]{:S(2)}) %collective-permute-start.9) | collective-permute-done | bytes 294944 | tf_op jit(solution)/shard_map/ppermute | solution.py:87
  (69 shorter events, 18.9 us)
Async XLA Ops:
  8.6 74.0 %copy-start.2 = (s32[64]{0:T(128)S(1)}, s32[64]{0:T(128)}, u32[]{:S(2)}) copy-start(s32[64]{0:T(128)} %param.9) | copy-start | bytes 772
  8.6 74.3 %copy-start.1 = (s32[8192]{0:T(1024)S(1)}, s32[8192]{0:T(1024)}, u32[]{:S(2)}) copy-start(s32[8192]{0:T(1024)} %param.10) | copy-start | bytes 98308
  9.4 65.8 %all-to-all-start.1 = ((bf16[16,32,256]{2,1,0:T(8,128)(2,1)}), bf16[16,32,256]{2,1,0:T(8,128)(2,1)S(1)}, u32[]{:S(2)}, u32[]{:S(2)}) async-start(bf16[16,32,256]{2,1,0:T(8,128)(2,1)} %get-tuple-element.27), calls=%async_computation.1 | async-start | bytes 524288 | tf_op jit(solution)/shard_map/all_to_all | solution.py:68
  37.4 50.6 %collective-permute-start = (bf16[128,2048]{0,1:T(8,128)(2,1)}, bf16[128,2048]{0,1:T(8,128)(2,1)S(1)}, u32[]{:S(2)}, u32[]{:S(2)}) collective-permute-start(bf16[128,2048]{0,1:T(8,128)(2,1)} %get-tuple-element.9), channel_id=1, source_target_pairs={{0,4},{4,8},{8,12},{12,0},{1,5},{5,9},{9,13},{13,1},{2,6},{6,10},{... | collective-permute-start | bytes 1572872 | tf_op jit(solution)/shard_map/ppermute | solution.py:58
  40.8 53.4 %collective-permute-start.1 = (bf16[128,2048]{0,1:T(8,128)(2,1)}, bf16[128,2048]{0,1:T(8,128)(2,1)S(1)}, u32[]{:S(2)}, u32[]{:S(2)}) collective-permute-start(bf16[128,2048]{0,1:T(8,128)(2,1)} %get-tuple-element.10), channel_id=1, source_target_pairs={{0,8},{4,12},{8,0},{12,4},{1,9},{5,13},{9,1},{13,5},{2,10},{6,14},... | collective-permute-start | bytes 1572872 | tf_op jit(solution)/shard_map/ppermute | solution.py:58
  43.8 77.6 %collective-permute-start.2 = (bf16[128,2048]{0,1:T(8,128)(2,1)}, bf16[128,2048]{0,1:T(8,128)(2,1)S(1)}, u32[]{:S(2)}, u32[]{:S(2)}) collective-permute-start(bf16[128,2048]{0,1:T(8,128)(2,1)} %get-tuple-element.11), channel_id=1, source_target_pairs={{0,12},{4,0},{8,4},{12,8},{1,13},{5,1},{9,5},{13,9},{2,14},{6,2},{... | collective-permute-start | bytes 1572872 | tf_op jit(solution)/shard_map/ppermute | solution.py:58
  75.1 44.3 %all-to-all-start = ((bf16[16,32,256]{2,1,0:T(8,128)(2,1)}), bf16[16,32,256]{2,1,0:T(8,128)(2,1)S(1)}, u32[]{:S(2)}, u32[]{:S(2)}) async-start(bf16[16,32,256]{2,1,0:T(8,128)(2,1)} %get-tuple-element.28), calls=%async_computation | async-start | bytes 524288 | tf_op jit(solution)/shard_map/all_to_all | solution.py:68
  84.1 42.3 %collective-permute-start.8 = (bf16[16,32,256]{2,1,0:T(8,128)(2,1)S(1)}, bf16[16,32,256]{2,1,0:T(8,128)(2,1)S(1)}, u32[]{:S(2)}, u32[]{:S(2)}) collective-permute-start(bf16[16,32,256]{2,1,0:T(8,128)(2,1)S(1)} %all-to-all-done.1), channel_id=1, source_target_pairs={{0,48},{16,32},{32,16},{48,0},{1,49},{17,33},{33,17},{49,1},{2,50}... | collective-permute-start | bytes 786440 | tf_op jit(solution)/shard_map/ppermute | solution.py:72
  88.9 41.9 %collective-permute-start.7 = (bf16[16,32,256]{2,1,0:T(8,128)(2,1)S(1)}, bf16[16,32,256]{2,1,0:T(8,128)(2,1)S(1)}, u32[]{:S(2)}, u32[]{:S(2)}) collective-permute-start(bf16[16,32,256]{2,1,0:T(8,128)(2,1)S(1)} %all-to-all-done.1), channel_id=1, source_target_pairs={{0,32},{16,48},{32,0},{48,16},{1,33},{17,49},{33,1},{49,17},{2,34}... | collective-permute-start | bytes 786440 | tf_op jit(solution)/shard_map/ppermute | solution.py:72
  91.8 39.0 %collective-permute-start.6 = (bf16[16,32,256]{2,1,0:T(8,128)(2,1)S(1)}, bf16[16,32,256]{2,1,0:T(8,128)(2,1)S(1)}, u32[]{:S(2)}, u32[]{:S(2)}) collective-permute-start(bf16[16,32,256]{2,1,0:T(8,128)(2,1)S(1)} %all-to-all-done.1), channel_id=1, source_target_pairs={{0,16},{16,0},{32,48},{48,32},{1,17},{17,1},{33,49},{49,33},{2,18}... | collective-permute-start | bytes 786440 | tf_op jit(solution)/shard_map/ppermute | solution.py:72
  119.5 12.1 %collective-permute-start.5 = (bf16[16,32,256]{2,1,0:T(8,128)(2,1)S(1)}, bf16[16,32,256]{2,1,0:T(8,128)(2,1)}, u32[]{:S(2)}, u32[]{:S(2)}) collective-permute-start(bf16[16,32,256]{2,1,0:T(8,128)(2,1)S(1)} %all-to-all-done), channel_id=1, source_target_pairs={{0,48},{16,32},{32,16},{48,0},{1,49},{17,33},{33,17},{49,1},{2,50}... | collective-permute-start | bytes 786440 | tf_op jit(solution)/shard_map/ppermute | solution.py:72
  121.4 12.9 %collective-permute-start.4 = (bf16[16,32,256]{2,1,0:T(8,128)(2,1)S(1)}, bf16[16,32,256]{2,1,0:T(8,128)(2,1)}, u32[]{:S(2)}, u32[]{:S(2)}) collective-permute-start(bf16[16,32,256]{2,1,0:T(8,128)(2,1)S(1)} %all-to-all-done), channel_id=1, source_target_pairs={{0,32},{16,48},{32,0},{48,16},{1,33},{17,49},{33,1},{49,17},{2,34}... | collective-permute-start | bytes 786440 | tf_op jit(solution)/shard_map/ppermute | solution.py:72
  126.4 9.3 %collective-permute-start.3 = (bf16[16,32,256]{2,1,0:T(8,128)(2,1)S(1)}, bf16[16,32,256]{2,1,0:T(8,128)(2,1)}, u32[]{:S(2)}, u32[]{:S(2)}) collective-permute-start(bf16[16,32,256]{2,1,0:T(8,128)(2,1)S(1)} %all-to-all-done), channel_id=1, source_target_pairs={{0,16},{16,0},{32,48},{48,32},{1,17},{17,1},{33,49},{49,33},{2,18}... | collective-permute-start | bytes 786440 | tf_op jit(solution)/shard_map/ppermute | solution.py:72
  137.5 1.7 %copy-start = (bf16[576,2048]{0,1:T(8,128)(2,1)S(1)}, bf16[576,2048]{0,1:T(8,128)(2,1)}, u32[]{:S(2)}) copy-start(bf16[576,2048]{0,1:T(8,128)(2,1)} %constant_dynamic-update-slice_fusion) | copy-start | bytes 7077892
  143.6 10.9 %collective-permute-start.11 = (f32[576,128]{1,0:T(8,128)S(1)}, f32[576,128]{1,0:T(8,128)S(1)}, u32[]{:S(2)}, u32[]{:S(2)}) collective-permute-start(f32[576,128]{1,0:T(8,128)S(1)} %bitcast.90), channel_id=1, source_target_pairs={{0,4},{4,8},{8,12},{12,0},{1,5},{5,9},{9,13},{13,1},{2,6},{6,10},{... | collective-permute-start | bytes 884744 | tf_op jit(solution)/shard_map/ppermute | solution.py:87
  147.0 13.3 %collective-permute-start.10 = (f32[576,128]{1,0:T(8,128)S(1)}, f32[576,128]{1,0:T(8,128)S(1)}, u32[]{:S(2)}, u32[]{:S(2)}) collective-permute-start(f32[576,128]{1,0:T(8,128)S(1)} %bitcast.88), channel_id=1, source_target_pairs={{0,8},{4,12},{8,0},{12,4},{1,9},{5,13},{9,1},{13,5},{2,10},{6,14},... | collective-permute-start | bytes 884744 | tf_op jit(solution)/shard_map/ppermute | solution.py:87
  150.1 13.5 %collective-permute-start.9 = (f32[576,128]{1,0:T(8,128)S(1)}, f32[576,128]{1,0:T(8,128)S(1)}, u32[]{:S(2)}, u32[]{:S(2)}) collective-permute-start(f32[576,128]{1,0:T(8,128)S(1)} %bitcast.86), channel_id=1, source_target_pairs={{0,12},{4,0},{8,4},{12,8},{1,13},{5,1},{9,5},{13,9},{2,14},{6,2},{... | collective-permute-start | bytes 884744 | tf_op jit(solution)/shard_map/ppermute | solution.py:87

commit v5 on v3

--- a/solution.py
+++ b/solution.py
@@ -46,8 +46,14 @@
     sign_rows = jnp.eye(blocks_all, dtype=jnp.float32)[:, :, None] * own_signs[None, :, :]
     sign_rows = sign_rows.reshape(blocks_all, blocks_all * quarter).astype(jnp.bfloat16)
 
-    send, normed_send = lax.optimization_barrier((send, normed_send))
-    normed_recv = lax.all_to_all(normed_send, "rep", 0, 0, tiled=True)
+    chunks = [
+        lax.dynamic_index_in_dim(normed_send, (replica + k) % n_rep, 0, keepdims=False)
+        for k in range(n_rep)
+    ]
+    normed_got = [chunks[0]]
+    for k in range(1, n_rep):
+        pairs = [(i, (i + k) % n_rep) for i in range(n_rep)]
+        normed_got.append(lax.ppermute(chunks[k], "rep", pairs))
     recv = lax.all_to_all(send, "ft", 0, 0, tiled=True)
     shared = [recv]
     for shift in range(1, n_fs):
@@ -65,7 +71,7 @@
     ordered = ordered.reshape(blocks_all * quarter, 2 * rank_width)
 
     lhs = jnp.concatenate(
-        [normed_recv.reshape(n_rep * probe_rows, blocks_all * quarter), sign_rows], axis=0
+        [*normed_got, sign_rows], axis=0
     )
     partial = jnp.dot(lhs, ordered, preferred_element_type=jnp.float32)
     hidden_part = partial[: n_rep * probe_rows].reshape(n_rep, probe_rows * 2 * rank_width)
@@ -74,7 +80,12 @@
     digest_part = jnp.broadcast_to(digest_part.reshape(1, -1), (n_rep, blocks_all * 2 * narrow))
     lanes = 128
     packed = jnp.concatenate([hidden_part, digest_part], axis=1).reshape(n_rep, -1, lanes)
-    pieces = lax.all_to_all(packed, "rep", 0, 0, tiled=True)
+    back = [packed[0]]
+    for k in range(1, n_rep):
+        pairs = [(i, (i - k) % n_rep) for i in range(n_rep)]
+        back.append(lax.ppermute(packed[k], "rep", pairs))
+    slot_of = (jnp.arange(n_rep, dtype=jnp.int32) - replica) % n_rep
+    pieces = jnp.take(jnp.stack(back), slot_of, axis=0)
     summed = pieces[0]
     for other in range(1, n_rep):
         summed = summed + pieces[other]

time: 164 us -> 153 us (0.933)
  the two profiles are of different devices: /device:TPU:64 before, /device:TPU:72 now
where the time goes in v5:
time: 153 us; the launch traced here: 152 us
  waiting for transfers between devices  63.2 us (41%)
  starting transfers between devices  58.7 us (38%)
  local copies, waits for them, and re-layouts  20.4 us (13%)
  other arithmetic  7.54 us (5%)
    all_to_all x1, waiting for transfers between devices, on_device(): recv = lax.all_to_all(send, 'ft', 0, 0, tiled=True)  37.9 us
    all_to_all x1, starting transfers between devices, on_device(): recv = lax.all_to_all(send, 'ft', 0, 0, tiled=True)  28 us
    ppermute x3, waiting for transfers between devices, on_device(): shared.append(lax.ppermute(recv, 'fs', pairs))  13.8 us
    unnamed x13, local copies, waits for them, and re-layouts  11.6 us
    ppermute x3, waiting for transfers between devices, on_device(): back.append(lax.ppermute(packed[k], 'rep', pairs))  11.5 us
    ppermute x3, starting transfers between devices, on_device(): normed_got.append(lax.ppermute(chunks[k], 'rep', pairs))  11.4 us
    ppermute x3, starting transfers between devices, on_device(): back.append(lax.ppermute(packed[k], 'rep', pairs))  10.2 us
    ppermute x3, starting transfers between devices, on_device(): shared.append(lax.ppermute(recv, 'fs', pairs))  9.2 us
  transfers between devices with their start and end apart: 10, of which 6 were waited for; matrix products, arithmetic and copies ran while one was open for 10% of the time, Pallas kernels for 0%

profile of v5, /device:TPU:72, one launch (start us, length us, event | category | flops | bytes accessed | tf_op | source)
XLA Modules:
  0.0 152.3 jit_solution(14710517820159472411)
XLA Ops:
  3.4 28.0 %all-to-all-start = ((bf16[16,32,512]{2,1,0:T(8,128)(2,1)}), bf16[16,32,512]{2,1,0:T(8,128)(2,1)S(1)}, u32[]{:S(2)}, u32[]{:S(2)}) async-start(bf16[16,32,512]{2,1,0:T(8,128)(2,1)} %reshape.237), calls=%async_computation | async-start | bytes 1048576 | tf_op jit(solution)/shard_map/all_to_all | solution.py:57
  31.4 3.2 %copy.16 = bf16[1,1,128,8192]{2,3,1,0:T(8,128)(2,1)S(1)} copy(bf16[1,1,128,8192]{3,2,1,0:T(8,128)(2,1)} %param.9) | data formatting | bytes 4194304 | tf_op args[4]
  37.9 3.4 %collective-permute-start = (bf16[128,2048]{0,1:T(8,128)(2,1)}, bf16[128,2048]{0,1:T(8,128)(2,1)}, u32[]{:S(2)}, u32[]{:S(2)}) collective-permute-start(bf16[128,2048]{0,1:T(8,128)(2,1)} %get-tuple-element.10), channel_id=1, source_target_pairs={{0,4},{4,8},{8,12},{12,0},{1,5},{5,9},{9,13},{13,1},{2,6},{6,10},{... | collective-permute-start | bytes 1572872 | tf_op jit(solution)/shard_map/ppermute | solution.py:56
  41.3 4.6 %collective-permute-start.1 = (bf16[128,2048]{0,1:T(8,128)(2,1)}, bf16[128,2048]{0,1:T(8,128)(2,1)}, u32[]{:S(2)}, u32[]{:S(2)}) collective-permute-start(bf16[128,2048]{0,1:T(8,128)(2,1)} %get-tuple-element.9), channel_id=1, source_target_pairs={{0,8},{4,12},{8,0},{12,4},{1,9},{5,13},{9,1},{13,5},{2,10},{6,14},... | collective-permute-start | bytes 1572872 | tf_op jit(solution)/shard_map/ppermute | solution.py:56
  45.9 3.3 %collective-permute-start.2 = (bf16[128,2048]{0,1:T(8,128)(2,1)S(1)}, bf16[128,2048]{0,1:T(8,128)(2,1)}, u32[]{:S(2)}, u32[]{:S(2)}) collective-permute-start(bf16[128,2048]{0,1:T(8,128)(2,1)S(1)} %get-tuple-element.8), channel_id=1, source_target_pairs={{0,12},{4,0},{8,4},{12,8},{1,13},{5,1},{9,5},{13,9},{2,14},{6,2},{... | collective-permute-start | bytes 1572872 | tf_op jit(solution)/shard_map/ppermute | solution.py:56
  51.2 37.9 %all-to-all-done = bf16[16,32,512]{2,1,0:T(8,128)(2,1)S(1)} async-done(((bf16[16,32,512]{2,1,0:T(8,128)(2,1)}), bf16[16,32,512]{2,1,0:T(8,128)(2,1)S(1)}, u32[]{:S(2)}, u32[]{:S(2)}) %all-to-all-start) | async-done | bytes 524320 | tf_op jit(solution)/shard_map/all_to_all | solution.py:57
  89.1 2.3 %collective-permute-start.3 = (bf16[16,32,512]{2,1,0:T(8,128)(2,1)S(1)}, bf16[16,32,512]{2,1,0:T(8,128)(2,1)S(1)}, u32[]{:S(2)}, u32[]{:S(2)}) collective-permute-start(bf16[16,32,512]{2,1,0:T(8,128)(2,1)S(1)} %all-to-all-done), channel_id=1, source_target_pairs={{0,16},{16,0},{32,48},{48,32},{1,17},{17,1},{33,49},{49,33},{2,18}... | collective-permute-start | bytes 1572872 | tf_op jit(solution)/shard_map/ppermute | solution.py:61
  91.5 1.9 %collective-permute-start.4 = (bf16[16,32,512]{2,1,0:T(8,128)(2,1)S(1)}, bf16[16,32,512]{2,1,0:T(8,128)(2,1)S(1)}, u32[]{:S(2)}, u32[]{:S(2)}) collective-permute-start(bf16[16,32,512]{2,1,0:T(8,128)(2,1)S(1)} %all-to-all-done), channel_id=1, source_target_pairs={{0,32},{16,48},{32,0},{48,16},{1,33},{17,49},{33,1},{49,17},{2,34}... | collective-permute-start | bytes 1572872 | tf_op jit(solution)/shard_map/ppermute | solution.py:61
  93.4 4.9 %collective-permute-start.5 = (bf16[16,32,512]{2,1,0:T(8,128)(2,1)S(1)}, bf16[16,32,512]{2,1,0:T(8,128)(2,1)S(1)}, u32[]{:S(2)}, u32[]{:S(2)}) collective-permute-start(bf16[16,32,512]{2,1,0:T(8,128)(2,1)S(1)} %all-to-all-done), channel_id=1, source_target_pairs={{0,48},{16,32},{32,16},{48,0},{1,49},{17,33},{33,17},{49,1},{2,50}... | collective-permute-start | bytes 1572872 | tf_op jit(solution)/shard_map/ppermute | solution.py:61
  98.4 1.9 %constant_dynamic-update-slice_fusion.3 = bf16[576,2048]{0,1:T(8,128)(2,1)} fusion(bf16[576,2048]{0,1:T(8,128)(2,1)} %bitcast_dynamic-update-slice_fusion, bf16[128,2048]{0,1:T(8,128)(2,1)} %collective-permute-done), kind=kLoop, calls=%fused_computation.39 | loop fusion | bytes 1048576
  100.3 1.9 %constant_dynamic-update-slice_fusion.2 = bf16[576,2048]{0,1:T(8,128)(2,1)} fusion(bf16[576,2048]{0,1:T(8,128)(2,1)} %constant_dynamic-update-slice_fusion.3, bf16[128,2048]{0,1:T(8,128)(2,1)} %collective-permute-done.1), kind=kLoop, calls=%fused_computation.38 | loop fusion | bytes 1048576
  102.2 1.9 %constant_dynamic-update-slice_fusion.1 = bf16[576,2048]{0,1:T(8,128)(2,1)} fusion(bf16[576,2048]{0,1:T(8,128)(2,1)} %constant_dynamic-update-slice_fusion.2, bf16[128,2048]{0,1:T(8,128)(2,1)} %collective-permute-done.2), kind=kLoop, calls=%fused_computation.37 | loop fusion | bytes 1048576
  104.1 1.2 constant_dynamic-update-slice_fusion
  105.3 2.9 %collective-permute-done.4 = bf16[16,32,512]{2,1,0:T(8,128)(2,1)S(1)} collective-permute-done((bf16[16,32,512]{2,1,0:T(8,128)(2,1)S(1)}, bf16[16,32,512]{2,1,0:T(8,128)(2,1)S(1)}, u32[]{:S(2)}, u32[]{:S(2)}) %collective-permute-start.4) | collective-permute-done | bytes 524320 | tf_op jit(solution)/shard_map/ppermute | solution.py:61
  108.2 10.9 %collective-permute-done.5 = bf16[16,32,512]{2,1,0:T(8,128)(2,1)S(1)} collective-permute-done((bf16[16,32,512]{2,1,0:T(8,128)(2,1)S(1)}, bf16[16,32,512]{2,1,0:T(8,128)(2,1)S(1)}, u32[]{:S(2)}, u32[]{:S(2)}) %collective-permute-start.5) | collective-permute-done | bytes 524320 | tf_op jit(solution)/shard_map/ppermute | solution.py:61
  119.3 2.0 %gather_fusion = bf16[64,32,512]{2,1,0:T(8,128)(2,1)} fusion(bf16[64,32,512]{2,1,0:T(8,128)(2,1)S(1)} %bitcast.67, s32[1024]{0:T(1024)S(1)} %pad_clamp_fusion.1), kind=kCustom, calls=%fused_computation | custom fusion | bytes 4194560 | tf_op jit(solution)/shard_map/jit(_take)/gather | solution.py:70
  121.3 1.9 %bitcast_select_fusion = bf16[2048,512]{1,0:T(8,128)(2,1)S(1)} fusion(bf16[64,32,512]{2,1,0:T(8,128)(2,1)} %gather_fusion, pred[2048]{0:T(1024)(128)(4,1)S(1)} %broadcast_in_dim.64), kind=kLoop, calls=%fused_computation.7 | loop fusion | flops 1048576 | bytes 4196352 | tf_op jit(solution)/shard_map/jit(_take)/select_n | solution.py:70
  123.7 1.4 fusion.11
  127.7 4.7 %collective-permute-start.6 = (f32[576,128]{1,0:T(8,128)S(1)}, f32[576,128]{1,0:T(8,128)S(1)}, u32[]{:S(2)}, u32[]{:S(2)}) collective-permute-start(f32[576,128]{1,0:T(8,128)S(1)} %bitcast.80), channel_id=1, source_target_pairs={{0,12},{4,0},{8,4},{12,8},{1,13},{5,1},{9,5},{13,9},{2,14},{6,2},{... | collective-permute-start | bytes 884744 | tf_op jit(solution)/shard_map/ppermute | solution.py:86
  132.3 2.7 %collective-permute-start.7 = (f32[576,128]{1,0:T(8,128)S(1)}, f32[576,128]{1,0:T(8,128)S(1)}, u32[]{:S(2)}, u32[]{:S(2)}) collective-permute-start(f32[576,128]{1,0:T(8,128)S(1)} %bitcast.78), channel_id=1, source_target_pairs={{0,8},{4,12},{8,0},{12,4},{1,9},{5,13},{9,1},{13,5},{2,10},{6,14},... | collective-permute-start | bytes 884744 | tf_op jit(solution)/shard_map/ppermute | solution.py:86
  135.0 2.8 %collective-permute-start.8 = (f32[576,128]{1,0:T(8,128)S(1)}, f32[576,128]{1,0:T(8,128)S(1)}, u32[]{:S(2)}, u32[]{:S(2)}) collective-permute-start(f32[576,128]{1,0:T(8,128)S(1)} %bitcast.76), channel_id=1, source_target_pairs={{0,4},{4,8},{8,12},{12,0},{1,5},{5,9},{9,13},{13,1},{2,6},{6,10},{... | collective-permute-start | bytes 884744 | tf_op jit(solution)/shard_map/ppermute | solution.py:86
  137.9 5.9 %collective-permute-done.6 = f32[576,128]{1,0:T(8,128)S(1)} collective-permute-done((f32[576,128]{1,0:T(8,128)S(1)}, f32[576,128]{1,0:T(8,128)S(1)}, u32[]{:S(2)}, u32[]{:S(2)}) %collective-permute-start.6) | collective-permute-done | bytes 294944 | tf_op jit(solution)/shard_map/ppermute | solution.py:86
  143.8 1.8 %collective-permute-done.7 = f32[576,128]{1,0:T(8,128)S(1)} collective-permute-done((f32[576,128]{1,0:T(8,128)S(1)}, f32[576,128]{1,0:T(8,128)S(1)}, u32[]{:S(2)}, u32[]{:S(2)}) %collective-permute-start.7) | collective-permute-done | bytes 294944 | tf_op jit(solution)/shard_map/ppermute | solution.py:86
  145.6 3.8 %collective-permute-done.8 = f32[576,128]{1,0:T(8,128)S(1)} collective-permute-done((f32[576,128]{1,0:T(8,128)S(1)}, f32[576,128]{1,0:T(8,128)S(1)}, u32[]{:S(2)}, u32[]{:S(2)}) %collective-permute-start.8) | collective-permute-done | bytes 294944 | tf_op jit(solution)/shard_map/ppermute | solution.py:86
  (59 shorter events, 13.9 us)
Async XLA Ops:
  3.4 85.7 %all-to-all-start = ((bf16[16,32,512]{2,1,0:T(8,128)(2,1)}), bf16[16,32,512]{2,1,0:T(8,128)(2,1)S(1)}, u32[]{:S(2)}, u32[]{:S(2)}) async-start(bf16[16,32,512]{2,1,0:T(8,128)(2,1)} %reshape.237), calls=%async_computation | async-start | bytes 1048576 | tf_op jit(solution)/shard_map/all_to_all | solution.py:57
  36.7 12.7 %copy-start.2 = (s32[64]{0:T(128)S(1)}, s32[64]{0:T(128)}, u32[]{:S(2)}) copy-start(s32[64]{0:T(128)} %param.7) | copy-start | bytes 772
  36.8 13.0 %copy-start.1 = (s32[8192]{0:T(1024)S(1)}, s32[8192]{0:T(1024)}, u32[]{:S(2)}) copy-start(s32[8192]{0:T(1024)} %param.8) | copy-start | bytes 98308
  37.9 55.5 %collective-permute-start = (bf16[128,2048]{0,1:T(8,128)(2,1)}, bf16[128,2048]{0,1:T(8,128)(2,1)}, u32[]{:S(2)}, u32[]{:S(2)}) collective-permute-start(bf16[128,2048]{0,1:T(8,128)(2,1)} %get-tuple-element.10), channel_id=1, source_target_pairs={{0,4},{4,8},{8,12},{12,0},{1,5},{5,9},{9,13},{13,1},{2,6},{6,10},{... | collective-permute-start | bytes 1572872 | tf_op jit(solution)/shard_map/ppermute | solution.py:56
  41.3 59.0 %collective-permute-start.1 = (bf16[128,2048]{0,1:T(8,128)(2,1)}, bf16[128,2048]{0,1:T(8,128)(2,1)}, u32[]{:S(2)}, u32[]{:S(2)}) collective-permute-start(bf16[128,2048]{0,1:T(8,128)(2,1)} %get-tuple-element.9), channel_id=1, source_target_pairs={{0,8},{4,12},{8,0},{12,4},{1,9},{5,13},{9,1},{13,5},{2,10},{6,14},... | collective-permute-start | bytes 1572872 | tf_op jit(solution)/shard_map/ppermute | solution.py:56
  45.9 56.3 %collective-permute-start.2 = (bf16[128,2048]{0,1:T(8,128)(2,1)S(1)}, bf16[128,2048]{0,1:T(8,128)(2,1)}, u32[]{:S(2)}, u32[]{:S(2)}) collective-permute-start(bf16[128,2048]{0,1:T(8,128)(2,1)S(1)} %get-tuple-element.8), channel_id=1, source_target_pairs={{0,12},{4,0},{8,4},{12,8},{1,13},{5,1},{9,5},{13,9},{2,14},{6,2},{... | collective-permute-start | bytes 1572872 | tf_op jit(solution)/shard_map/ppermute | solution.py:56
  89.1 16.2 %collective-permute-start.3 = (bf16[16,32,512]{2,1,0:T(8,128)(2,1)S(1)}, bf16[16,32,512]{2,1,0:T(8,128)(2,1)S(1)}, u32[]{:S(2)}, u32[]{:S(2)}) collective-permute-start(bf16[16,32,512]{2,1,0:T(8,128)(2,1)S(1)} %all-to-all-done), channel_id=1, source_target_pairs={{0,16},{16,0},{32,48},{48,32},{1,17},{17,1},{33,49},{49,33},{2,18}... | collective-permute-start | bytes 1572872 | tf_op jit(solution)/shard_map/ppermute | solution.py:61
  91.5 16.7 %collective-permute-start.4 = (bf16[16,32,512]{2,1,0:T(8,128)(2,1)S(1)}, bf16[16,32,512]{2,1,0:T(8,128)(2,1)S(1)}, u32[]{:S(2)}, u32[]{:S(2)}) collective-permute-start(bf16[16,32,512]{2,1,0:T(8,128)(2,1)S(1)} %all-to-all-done), channel_id=1, source_target_pairs={{0,32},{16,48},{32,0},{48,16},{1,33},{17,49},{33,1},{49,17},{2,34}... | collective-permute-start | bytes 1572872 | tf_op jit(solution)/shard_map/ppermute | solution.py:61
  93.4 25.6 %collective-permute-start.5 = (bf16[16,32,512]{2,1,0:T(8,128)(2,1)S(1)}, bf16[16,32,512]{2,1,0:T(8,128)(2,1)S(1)}, u32[]{:S(2)}, u32[]{:S(2)}) collective-permute-start(bf16[16,32,512]{2,1,0:T(8,128)(2,1)S(1)} %all-to-all-done), channel_id=1, source_target_pairs={{0,48},{16,32},{32,16},{48,0},{1,49},{17,33},{33,17},{49,1},{2,50}... | collective-permute-start | bytes 1572872 | tf_op jit(solution)/shard_map/ppermute | solution.py:61
  121.3 2.4 %copy-start = (bf16[576,2048]{0,1:T(8,128)(2,1)S(1)}, bf16[576,2048]{0,1:T(8,128)(2,1)}, u32[]{:S(2)}) copy-start(bf16[576,2048]{0,1:T(8,128)(2,1)} %constant_dynamic-update-slice_fusion) | copy-start | bytes 7077892
  127.7 16.2 %collective-permute-start.6 = (f32[576,128]{1,0:T(8,128)S(1)}, f32[576,128]{1,0:T(8,128)S(1)}, u32[]{:S(2)}, u32[]{:S(2)}) collective-permute-start(f32[576,128]{1,0:T(8,128)S(1)} %bitcast.80), channel_id=1, source_target_pairs={{0,12},{4,0},{8,4},{12,8},{1,13},{5,1},{9,5},{13,9},{2,14},{6,2},{... | collective-permute-start | bytes 884744 | tf_op jit(solution)/shard_map/ppermute | solution.py:86
  132.3 13.3 %collective-permute-start.7 = (f32[576,128]{1,0:T(8,128)S(1)}, f32[576,128]{1,0:T(8,128)S(1)}, u32[]{:S(2)}, u32[]{:S(2)}) collective-permute-start(f32[576,128]{1,0:T(8,128)S(1)} %bitcast.78), channel_id=1, source_target_pairs={{0,8},{4,12},{8,0},{12,4},{1,9},{5,13},{9,1},{13,5},{2,10},{6,14},... | collective-permute-start | bytes 884744 | tf_op jit(solution)/shard_map/ppermute | solution.py:86
  135.0 14.4 %collective-permute-start.8 = (f32[576,128]{1,0:T(8,128)S(1)}, f32[576,128]{1,0:T(8,128)S(1)}, u32[]{:S(2)}, u32[]{:S(2)}) collective-permute-start(f32[576,128]{1,0:T(8,128)S(1)} %bitcast.76), channel_id=1, source_target_pairs={{0,4},{4,8},{8,12},{12,0},{1,5},{5,9},{9,13},{13,1},{2,6},{6,10},{... | collective-permute-start | bytes 884744 | tf_op jit(solution)/shard_map/ppermute | solution.py:86

commit v6 on v5

--- a/solution.py
+++ b/solution.py
@@ -29,11 +29,6 @@
     send = mine.reshape(2, n_fs, piece, n_ft, rank_width).transpose(3, 1, 2, 0, 4)
     send = send.reshape(n_ft, n_fs * piece, 2 * rank_width)
 
-    positions = jnp.arange(blocks_all, dtype=jnp.int32)
-    inverse = jnp.sum(
-        jnp.where(owner_map[None, :] == positions[:, None], positions[None, :], 0), axis=1
-    )
-
     probe_rows = probes.shape[2]
     wide = probes.reshape(probe_rows, total_rows).astype(jnp.float32)
     meansq = jnp.mean(wide * wide, axis=-1, keepdims=True)
@@ -59,21 +54,21 @@
     for shift in range(1, n_fs):
         pairs = [(i, i ^ shift) for i in range(n_fs)]
         shared.append(lax.ppermute(recv, "fs", pairs))
-    gathered = jnp.stack([shared[k] for k in range(n_fs)])
     source_of = sub ^ jnp.arange(n_fs, dtype=jnp.int32)
-    gathered = gathered.reshape(n_fs, n_ft, quarter, 2 * rank_width)
     block_src = (jnp.arange(n_ft, dtype=jnp.int32)[None, :] * n_fs + source_of[:, None]).reshape(-1)
-    gathered = gathered.reshape(n_fs * n_ft, quarter, 2 * rank_width)
-    where_block = jnp.sum(
-        jnp.where(block_src[None, :] == inverse[:, None], positions[None, :], 0), axis=1
-    )
-    ordered = jnp.take(gathered, where_block, axis=0)
-    ordered = ordered.reshape(blocks_all * quarter, 2 * rank_width)
-
-    lhs = jnp.concatenate(
-        [*normed_got, sign_rows], axis=0
-    )
-    partial = jnp.dot(lhs, ordered, preferred_element_type=jnp.float32)
+    true_of_slot = owner_map[block_src]
+    lhs = jnp.concatenate([*normed_got, sign_rows], axis=0)
+    lhs_rows = lhs.shape[0]
+    lhs = jnp.take(lhs.reshape(lhs_rows, blocks_all, quarter), true_of_slot, axis=1)
+    lhs = lhs.reshape(lhs_rows, n_fs, n_ft * quarter)
+    partial = None
+    for k in range(n_fs):
+        term = jnp.dot(
+            lhs[:, k],
+            shared[k].reshape(n_ft * quarter, 2 * rank_width),
+            preferred_element_type=jnp.float32,
+        )
+        partial = term if partial is None else partial + term
     hidden_part = partial[: n_rep * probe_rows].reshape(n_rep, probe_rows * 2 * rank_width)
     digest_part = partial[n_rep * probe_rows :].reshape(blocks_all, 2, n_fs, narrow)
     digest_part = lax.dynamic_index_in_dim(digest_part, sub, 2, keepdims=False)

time: 153 us -> 147 us (0.961)
  the two profiles are of different devices: /device:TPU:72 before, /device:TPU:64 now
where the time goes in v6:
time: 147 us; the launch traced here: 146 us
  waiting for transfers between devices  60.6 us (41%)
  starting transfers between devices  58.7 us (40%)
  local copies, waits for them, and re-layouts  18.4 us (13%)
  other arithmetic  5.64 us (4%)
  matrix products  2.03 us (1%)
    all_to_all x1, starting transfers between devices, on_device(): recv = lax.all_to_all(send, 'ft', 0, 0, tiled=True)  28 us
    ppermute x3, waiting for transfers between devices, on_device(): shared.append(lax.ppermute(recv, 'fs', pairs))  16.9 us
    all_to_all x1, waiting for transfers between devices, on_device(): recv = lax.all_to_all(send, 'ft', 0, 0, tiled=True)  16.2 us
    ppermute x3, waiting for transfers between devices, on_device(): normed_got.append(lax.ppermute(chunks[k], 'rep', pairs))  14.7 us
    ppermute x3, waiting for transfers between devices, on_device(): back.append(lax.ppermute(packed[k], 'rep', pairs))  12.8 us
    ppermute x3, starting transfers between devices, on_device(): normed_got.append(lax.ppermute(chunks[k], 'rep', pairs))  11.4 us
    ppermute x3, starting transfers between devices, on_device(): back.append(lax.ppermute(packed[k], 'rep', pairs))  10.2 us
    ppermute x3, starting transfers between devices, on_device(): shared.append(lax.ppermute(recv, 'fs', pairs))  9.2 us
  transfers between devices with their start and end apart: 10, of which 9 were waited for; matrix products, arithmetic and copies ran while one was open for 12% of the time, Pallas kernels for 0%

profile of v6, /device:TPU:64, one launch (start us, length us, event | category | flops | bytes accessed | tf_op | source)
XLA Modules:
  0.0 146.4 jit_solution(6299632009634779409)
XLA Ops:
  0.7 1.1 fusion.5
  2.3 1.1 reshape.275
  3.4 28.0 %all-to-all-start = ((bf16[16,32,512]{2,1,0:T(8,128)(2,1)}), bf16[16,32,512]{2,1,0:T(8,128)(2,1)S(1)}, u32[]{:S(2)}, u32[]{:S(2)}) async-start(bf16[16,32,512]{2,1,0:T(8,128)(2,1)} %reshape.275), calls=%async_computation | async-start | bytes 1048576 | tf_op jit(solution)/shard_map/all_to_all | solution.py:52
  31.4 3.2 %copy.15 = bf16[1,1,128,8192]{2,3,1,0:T(8,128)(2,1)S(1)} copy(bf16[1,1,128,8192]{3,2,1,0:T(8,128)(2,1)} %param.9) | data formatting | bytes 4194304 | tf_op args[4]
  34.6 1.1 multiply_reduce_fusion
  36.8 1.2 dynamic-slice_bitcast_fusion
  38.0 3.4 %collective-permute-start = (bf16[128,2048]{0,1:T(8,128)(2,1)}, bf16[128,2048]{0,1:T(8,128)(2,1)S(1)}, u32[]{:S(2)}, u32[]{:S(2)}) collective-permute-start(bf16[128,2048]{0,1:T(8,128)(2,1)} %get-tuple-element.8), channel_id=1, source_target_pairs={{0,4},{4,8},{8,12},{12,0},{1,5},{5,9},{9,13},{13,1},{2,6},{6,10},{... | collective-permute-start | bytes 1572872 | tf_op jit(solution)/shard_map/ppermute | solution.py:51
  41.4 4.6 %collective-permute-start.1 = (bf16[128,2048]{0,1:T(8,128)(2,1)}, bf16[128,2048]{0,1:T(8,128)(2,1)S(1)}, u32[]{:S(2)}, u32[]{:S(2)}) collective-permute-start(bf16[128,2048]{0,1:T(8,128)(2,1)} %get-tuple-element.7), channel_id=1, source_target_pairs={{0,8},{4,12},{8,0},{12,4},{1,9},{5,13},{9,1},{13,5},{2,10},{6,14},... | collective-permute-start | bytes 1572872 | tf_op jit(solution)/shard_map/ppermute | solution.py:51
  46.0 3.3 %collective-permute-start.2 = (bf16[128,2048]{0,1:T(8,128)(2,1)}, bf16[128,2048]{0,1:T(8,128)(2,1)S(1)}, u32[]{:S(2)}, u32[]{:S(2)}) collective-permute-start(bf16[128,2048]{0,1:T(8,128)(2,1)} %get-tuple-element.6), channel_id=1, source_target_pairs={{0,12},{4,0},{8,4},{12,8},{1,13},{5,1},{9,5},{13,9},{2,14},{6,2},{... | collective-permute-start | bytes 1572872 | tf_op jit(solution)/shard_map/ppermute | solution.py:51
  51.7 3.4 %collective-permute-done = bf16[128,2048]{0,1:T(8,128)(2,1)S(1)} collective-permute-done((bf16[128,2048]{0,1:T(8,128)(2,1)}, bf16[128,2048]{0,1:T(8,128)(2,1)S(1)}, u32[]{:S(2)}, u32[]{:S(2)}) %collective-permute-start) | collective-permute-done | bytes 524320 | tf_op jit(solution)/shard_map/ppermute | solution.py:51
  56.0 10.6 %collective-permute-done.1 = bf16[128,2048]{0,1:T(8,128)(2,1)S(1)} collective-permute-done((bf16[128,2048]{0,1:T(8,128)(2,1)}, bf16[128,2048]{0,1:T(8,128)(2,1)S(1)}, u32[]{:S(2)}, u32[]{:S(2)}) %collective-permute-start.1) | collective-permute-done | bytes 524320 | tf_op jit(solution)/shard_map/ppermute | solution.py:51
  69.0 1.2 fusion.4
  70.2 2.7 %gather_fusion.1 = bf16[64,576,32]{1,2,0:T(8,128)(2,1)S(1)} fusion(bf16[576,64,32]{0,2,1:T(8,128)(2,1)} %fusion.4, s32[1024]{0:T(1024)S(1)} %pad_clamp_fusion.1), kind=kCustom, calls=%fused_computation.1 | custom fusion | bytes 4718848 | tf_op jit(solution)/shard_map/jit(_take)/gather | solution.py:62
  72.9 16.2 %all-to-all-done = bf16[16,32,512]{2,1,0:T(8,128)(2,1)S(1)} async-done(((bf16[16,32,512]{2,1,0:T(8,128)(2,1)}), bf16[16,32,512]{2,1,0:T(8,128)(2,1)S(1)}, u32[]{:S(2)}, u32[]{:S(2)}) %all-to-all-start) | async-done | bytes 524320 | tf_op jit(solution)/shard_map/all_to_all | solution.py:52
  89.1 1.9 %collective-permute-start.5 = (bf16[16,32,512]{2,1,0:T(8,128)(2,1)S(1)}, bf16[16,32,512]{2,1,0:T(8,128)(2,1)S(1)}, u32[]{:S(2)}, u32[]{:S(2)}) collective-permute-start(bf16[16,32,512]{2,1,0:T(8,128)(2,1)S(1)} %all-to-all-done), channel_id=1, source_target_pairs={{0,48},{16,32},{32,16},{48,0},{1,49},{17,33},{33,17},{49,1},{2,50}... | collective-permute-start | bytes 1572872 | tf_op jit(solution)/shard_map/ppermute | solution.py:56
  91.6 3.5 %collective-permute-start.3 = (bf16[16,32,512]{2,1,0:T(8,128)(2,1)S(1)}, bf16[16,32,512]{2,1,0:T(8,128)(2,1)S(1)}, u32[]{:S(2)}, u32[]{:S(2)}) collective-permute-start(bf16[16,32,512]{2,1,0:T(8,128)(2,1)S(1)} %all-to-all-done), channel_id=1, source_target_pairs={{0,16},{16,0},{32,48},{48,32},{1,17},{17,1},{33,49},{49,33},{2,18}... | collective-permute-start | bytes 1572872 | tf_op jit(solution)/shard_map/ppermute | solution.py:56
  95.1 3.8 %collective-permute-start.4 = (bf16[16,32,512]{2,1,0:T(8,128)(2,1)S(1)}, bf16[16,32,512]{2,1,0:T(8,128)(2,1)S(1)}, u32[]{:S(2)}, u32[]{:S(2)}) collective-permute-start(bf16[16,32,512]{2,1,0:T(8,128)(2,1)S(1)} %all-to-all-done), channel_id=1, source_target_pairs={{0,32},{16,48},{32,0},{48,16},{1,33},{17,49},{33,1},{49,17},{2,34}... | collective-permute-start | bytes 1572872 | tf_op jit(solution)/shard_map/ppermute | solution.py:56
  99.4 7.3 %collective-permute-done.5 = bf16[16,32,512]{2,1,0:T(8,128)(2,1)S(1)} collective-permute-done((bf16[16,32,512]{2,1,0:T(8,128)(2,1)S(1)}, bf16[16,32,512]{2,1,0:T(8,128)(2,1)S(1)}, u32[]{:S(2)}, u32[]{:S(2)}) %collective-permute-start.5) | collective-permute-done | bytes 524320 | tf_op jit(solution)/shard_map/ppermute | solution.py:56
  107.2 9.6 %collective-permute-done.3 = bf16[16,32,512]{2,1,0:T(8,128)(2,1)S(1)} collective-permute-done((bf16[16,32,512]{2,1,0:T(8,128)(2,1)S(1)}, bf16[16,32,512]{2,1,0:T(8,128)(2,1)S(1)}, u32[]{:S(2)}, u32[]{:S(2)}) %collective-permute-start.3) | collective-permute-done | bytes 524320 | tf_op jit(solution)/shard_map/ppermute | solution.py:56
  120.5 4.7 %collective-permute-start.6 = (f32[576,128]{1,0:T(8,128)S(1)}, f32[576,128]{1,0:T(8,128)S(1)}, u32[]{:S(2)}, u32[]{:S(2)}) collective-permute-start(f32[576,128]{1,0:T(8,128)S(1)} %bitcast.102), channel_id=1, source_target_pairs={{0,12},{4,0},{8,4},{12,8},{1,13},{5,1},{9,5},{13,9},{2,14},{6,2},{... | collective-permute-start | bytes 884744 | tf_op jit(solution)/shard_map/ppermute | solution.py:81
  125.1 2.7 %collective-permute-start.7 = (f32[576,128]{1,0:T(8,128)S(1)}, f32[576,128]{1,0:T(8,128)S(1)}, u32[]{:S(2)}, u32[]{:S(2)}) collective-permute-start(f32[576,128]{1,0:T(8,128)S(1)} %bitcast.100), channel_id=1, source_target_pairs={{0,8},{4,12},{8,0},{12,4},{1,9},{5,13},{9,1},{13,5},{2,10},{6,14},... | collective-permute-start | bytes 884744 | tf_op jit(solution)/shard_map/ppermute | solution.py:81
  127.9 2.8 %collective-permute-start.8 = (f32[576,128]{1,0:T(8,128)S(1)}, f32[576,128]{1,0:T(8,128)S(1)}, u32[]{:S(2)}, u32[]{:S(2)}) collective-permute-start(f32[576,128]{1,0:T(8,128)S(1)} %bitcast.98), channel_id=1, source_target_pairs={{0,4},{4,8},{8,12},{12,0},{1,5},{5,9},{9,13},{13,1},{2,6},{6,10},{... | collective-permute-start | bytes 884744 | tf_op jit(solution)/shard_map/ppermute | solution.py:81
  130.7 7.2 %collective-permute-done.6 = f32[576,128]{1,0:T(8,128)S(1)} collective-permute-done((f32[576,128]{1,0:T(8,128)S(1)}, f32[576,128]{1,0:T(8,128)S(1)}, u32[]{:S(2)}, u32[]{:S(2)}) %collective-permute-start.6) | collective-permute-done | bytes 294944 | tf_op jit(solution)/shard_map/ppermute | solution.py:81
  138.5 5.0 %collective-permute-done.8 = f32[576,128]{1,0:T(8,128)S(1)} collective-permute-done((f32[576,128]{1,0:T(8,128)S(1)}, f32[576,128]{1,0:T(8,128)S(1)}, u32[]{:S(2)}, u32[]{:S(2)}) %collective-permute-start.8) | collective-permute-done | bytes 294944 | tf_op jit(solution)/shard_map/ppermute | solution.py:81
  (60 shorter events, 15.7 us)
Async XLA Ops:
  0.6 48.9 %copy-start = (s32[64]{0:T(128)S(1)}, s32[64]{0:T(128)}, u32[]{:S(2)}) copy-start(s32[64]{0:T(128)} %param.7) | copy-start | bytes 772
  3.4 85.7 %all-to-all-start = ((bf16[16,32,512]{2,1,0:T(8,128)(2,1)}), bf16[16,32,512]{2,1,0:T(8,128)(2,1)S(1)}, u32[]{:S(2)}, u32[]{:S(2)}) async-start(bf16[16,32,512]{2,1,0:T(8,128)(2,1)} %reshape.275), calls=%async_computation | async-start | bytes 1048576 | tf_op jit(solution)/shard_map/all_to_all | solution.py:52
  36.8 13.7 %copy-start.1 = (s32[8192]{0:T(1024)S(1)}, s32[8192]{0:T(1024)}, u32[]{:S(2)}) copy-start(s32[8192]{0:T(1024)} %param.8) | copy-start | bytes 98308
  38.0 17.1 %collective-permute-start = (bf16[128,2048]{0,1:T(8,128)(2,1)}, bf16[128,2048]{0,1:T(8,128)(2,1)S(1)}, u32[]{:S(2)}, u32[]{:S(2)}) collective-permute-start(bf16[128,2048]{0,1:T(8,128)(2,1)} %get-tuple-element.8), channel_id=1, source_target_pairs={{0,4},{4,8},{8,12},{12,0},{1,5},{5,9},{9,13},{13,1},{2,6},{6,10},{... | collective-permute-start | bytes 1572872 | tf_op jit(solution)/shard_map/ppermute | solution.py:51
  41.4 25.2 %collective-permute-start.1 = (bf16[128,2048]{0,1:T(8,128)(2,1)}, bf16[128,2048]{0,1:T(8,128)(2,1)S(1)}, u32[]{:S(2)}, u32[]{:S(2)}) collective-permute-start(bf16[128,2048]{0,1:T(8,128)(2,1)} %get-tuple-element.7), channel_id=1, source_target_pairs={{0,8},{4,12},{8,0},{12,4},{1,9},{5,13},{9,1},{13,5},{2,10},{6,14},... | collective-permute-start | bytes 1572872 | tf_op jit(solution)/shard_map/ppermute | solution.py:51
  46.0 22.1 %collective-permute-start.2 = (bf16[128,2048]{0,1:T(8,128)(2,1)}, bf16[128,2048]{0,1:T(8,128)(2,1)S(1)}, u32[]{:S(2)}, u32[]{:S(2)}) collective-permute-start(bf16[128,2048]{0,1:T(8,128)(2,1)} %get-tuple-element.6), channel_id=1, source_target_pairs={{0,12},{4,0},{8,4},{12,8},{1,13},{5,1},{9,5},{13,9},{2,14},{6,2},{... | collective-permute-start | bytes 1572872 | tf_op jit(solution)/shard_map/ppermute | solution.py:51
  89.1 17.6 %collective-permute-start.5 = (bf16[16,32,512]{2,1,0:T(8,128)(2,1)S(1)}, bf16[16,32,512]{2,1,0:T(8,128)(2,1)S(1)}, u32[]{:S(2)}, u32[]{:S(2)}) collective-permute-start(bf16[16,32,512]{2,1,0:T(8,128)(2,1)S(1)} %all-to-all-done), channel_id=1, source_target_pairs={{0,48},{16,32},{32,16},{48,0},{1,49},{17,33},{33,17},{49,1},{2,50}... | collective-permute-start | bytes 1572872 | tf_op jit(solution)/shard_map/ppermute | solution.py:56
  91.6 25.2 %collective-permute-start.3 = (bf16[16,32,512]{2,1,0:T(8,128)(2,1)S(1)}, bf16[16,32,512]{2,1,0:T(8,128)(2,1)S(1)}, u32[]{:S(2)}, u32[]{:S(2)}) collective-permute-start(bf16[16,32,512]{2,1,0:T(8,128)(2,1)S(1)} %all-to-all-done), channel_id=1, source_target_pairs={{0,16},{16,0},{32,48},{48,32},{1,17},{17,1},{33,49},{49,33},{2,18}... | collective-permute-start | bytes 1572872 | tf_op jit(solution)/shard_map/ppermute | solution.py:56
  95.1 22.3 %collective-permute-start.4 = (bf16[16,32,512]{2,1,0:T(8,128)(2,1)S(1)}, bf16[16,32,512]{2,1,0:T(8,128)(2,1)S(1)}, u32[]{:S(2)}, u32[]{:S(2)}) collective-permute-start(bf16[16,32,512]{2,1,0:T(8,128)(2,1)S(1)} %all-to-all-done), channel_id=1, source_target_pairs={{0,32},{16,48},{32,0},{48,16},{1,33},{17,49},{33,1},{49,17},{2,34}... | collective-permute-start | bytes 1572872 | tf_op jit(solution)/shard_map/ppermute | solution.py:56
  120.5 17.5 %collective-permute-start.6 = (f32[576,128]{1,0:T(8,128)S(1)}, f32[576,128]{1,0:T(8,128)S(1)}, u32[]{:S(2)}, u32[]{:S(2)}) collective-permute-start(f32[576,128]{1,0:T(8,128)S(1)} %bitcast.102), channel_id=1, source_target_pairs={{0,12},{4,0},{8,4},{12,8},{1,13},{5,1},{9,5},{13,9},{2,14},{6,2},{... | collective-permute-start | bytes 884744 | tf_op jit(solution)/shard_map/ppermute | solution.py:81
  125.1 13.3 %collective-permute-start.7 = (f32[576,128]{1,0:T(8,128)S(1)}, f32[576,128]{1,0:T(8,128)S(1)}, u32[]{:S(2)}, u32[]{:S(2)}) collective-permute-start(f32[576,128]{1,0:T(8,128)S(1)} %bitcast.100), channel_id=1, source_target_pairs={{0,8},{4,12},{8,0},{12,4},{1,9},{5,13},{9,1},{13,5},{2,10},{6,14},... | collective-permute-start | bytes 884744 | tf_op jit(solution)/shard_map/ppermute | solution.py:81
  127.9 15.7 %collective-permute-start.8 = (f32[576,128]{1,0:T(8,128)S(1)}, f32[576,128]{1,0:T(8,128)S(1)}, u32[]{:S(2)}, u32[]{:S(2)}) collective-permute-start(f32[576,128]{1,0:T(8,128)S(1)} %bitcast.98), channel_id=1, source_target_pairs={{0,4},{4,8},{8,12},{12,0},{1,5},{5,9},{9,13},{13,1},{2,6},{6,10},{... | collective-permute-start | bytes 884744 | tf_op jit(solution)/shard_map/ppermute | solution.py:81

commit v7 on v6

--- a/solution.py
+++ b/solution.py
@@ -69,26 +69,31 @@
             preferred_element_type=jnp.float32,
         )
         partial = term if partial is None else partial + term
-    hidden_part = partial[: n_rep * probe_rows].reshape(n_rep, probe_rows * 2 * rank_width)
+    width2 = 2 * rank_width
+    hidden_part = partial[: n_rep * probe_rows].reshape(n_rep, probe_rows, width2)
     digest_part = partial[n_rep * probe_rows :].reshape(blocks_all, 2, n_fs, narrow)
     digest_part = lax.dynamic_index_in_dim(digest_part, sub, 2, keepdims=False)
-    digest_part = jnp.broadcast_to(digest_part.reshape(1, -1), (n_rep, blocks_all * 2 * narrow))
-    lanes = 128
-    packed = jnp.concatenate([hidden_part, digest_part], axis=1).reshape(n_rep, -1, lanes)
-    back = [packed[0]]
-    for k in range(1, n_rep):
-        pairs = [(i, (i - k) % n_rep) for i in range(n_rep)]
-        back.append(lax.ppermute(packed[k], "rep", pairs))
-    slot_of = (jnp.arange(n_rep, dtype=jnp.int32) - replica) % n_rep
-    pieces = jnp.take(jnp.stack(back), slot_of, axis=0)
-    summed = pieces[0]
-    for other in range(1, n_rep):
-        summed = summed + pieces[other]
-    summed = summed.reshape(-1)
-    hidden_sum = summed[: probe_rows * 2 * rank_width].reshape(probe_rows, 2, rank_width)
-    digest_sum = summed[probe_rows * 2 * rank_width :].reshape(blocks_all, 2, narrow)
+    digest_rows = digest_part.reshape(-1, width2)
+    back = []
+    for k in range(n_rep):
+        packed = jnp.concatenate([hidden_part[k], digest_rows], axis=0)
+        if k > 0:
+            pairs = [(i, (i - k) % n_rep) for i in range(n_rep)]
+            packed = lax.ppermute(packed, "rep", pairs)
+        back.append(packed)
+    if n_rep == 4:
+        summed = (back[0] + back[2]) + (back[1] + back[3])
+    else:
+        slot_of = (jnp.arange(n_rep, dtype=jnp.int32) - replica) % n_rep
+        pieces = jnp.take(jnp.stack(back), slot_of, axis=0)
+        summed = pieces[0]
+        for other in range(1, n_rep):
+            summed = summed + pieces[other]
+    hidden_sum = summed[:probe_rows]
+    digest_sum = summed[probe_rows:].reshape(blocks_all, 2, narrow)
     digest = 8.0 * digest_sum.transpose(1, 0, 2).reshape(2, blocks_all, 1, narrow)
-    hidden = (jax.nn.silu(hidden_sum[:, 0]) * hidden_sum[:, 1]).astype(jnp.bfloat16)
+    hidden = jax.nn.silu(hidden_sum[:, :rank_width]) * hidden_sum[:, rank_width:]
+    hidden = hidden.astype(jnp.bfloat16)
     return (digest, hidden.reshape(1, 1, probe_rows, 1, rank_width))
 
 

time: 147 us -> 140 us (0.952)
  the two profiles are of different devices: /device:TPU:64 before, /device:TPU:72 now
where the time goes in v7:
time: 140 us; the launch traced here: 139 us
  starting transfers between devices  59.4 us (42%)
  waiting for transfers between devices  56.4 us (40%)
  local copies, waits for them, and re-layouts  15.2 us (11%)
  other arithmetic  5.49 us (4%)
  matrix products  2.02 us (1%)
    all_to_all x1, starting transfers between devices, on_device(): recv = lax.all_to_all(send, 'ft', 0, 0, tiled=True)  28 us
    ppermute x3, waiting for transfers between devices, on_device(): shared.append(lax.ppermute(recv, 'fs', pairs))  16.9 us
    all_to_all x1, waiting for transfers between devices, on_device(): recv = lax.all_to_all(send, 'ft', 0, 0, tiled=True)  16.1 us
    ppermute x3, waiting for transfers between devices, on_device(): normed_got.append(lax.ppermute(chunks[k], 'rep', pairs))  14.7 us
    ppermute x3, starting transfers between devices, on_device(): normed_got.append(lax.ppermute(chunks[k], 'rep', pairs))  11.4 us
    ppermute x3, starting transfers between devices, on_device(): packed = lax.ppermute(packed, 'rep', pairs)  10.8 us
    ppermute x3, starting transfers between devices, on_device(): shared.append(lax.ppermute(recv, 'fs', pairs))  9.2 us
    ppermute x3, waiting for transfers between devices, on_device(): packed = lax.ppermute(packed, 'rep', pairs)  8.67 us
  transfers between devices with their start and end apart: 10, of which 9 were waited for; matrix products, arithmetic and copies ran while one was open for 12% of the time, Pallas kernels for 0%

profile of v7, /device:TPU:72, one launch (start us, length us, event | category | flops | bytes accessed | tf_op | source)
XLA Modules:
  0.0 139.4 jit_solution(3381706989144132901)
XLA Ops:
  0.7 1.1 fusion.5
  2.3 1.1 reshape.164
  3.4 28.0 %all-to-all-start = ((bf16[16,32,512]{2,1,0:T(8,128)(2,1)}), bf16[16,32,512]{2,1,0:T(8,128)(2,1)S(1)}, u32[]{:S(2)}, u32[]{:S(2)}) async-start(bf16[16,32,512]{2,1,0:T(8,128)(2,1)} %reshape.164), calls=%async_computation | async-start | bytes 1048576 | tf_op jit(solution)/shard_map/all_to_all | solution.py:52
  31.4 3.2 %copy.17 = bf16[1,1,128,8192]{2,3,1,0:T(8,128)(2,1)S(1)} copy(bf16[1,1,128,8192]{3,2,1,0:T(8,128)(2,1)} %param.9) | data formatting | bytes 4194304 | tf_op args[4]
  34.6 1.1 multiply_reduce_fusion
  36.8 1.2 dynamic-slice_bitcast_fusion
  38.0 3.4 %collective-permute-start = (bf16[128,2048]{0,1:T(8,128)(2,1)}, bf16[128,2048]{0,1:T(8,128)(2,1)S(1)}, u32[]{:S(2)}, u32[]{:S(2)}) collective-permute-start(bf16[128,2048]{0,1:T(8,128)(2,1)} %get-tuple-element.4), channel_id=1, source_target_pairs={{0,4},{4,8},{8,12},{12,0},{1,5},{5,9},{9,13},{13,1},{2,6},{6,10},{... | collective-permute-start | bytes 1572872 | tf_op jit(solution)/shard_map/ppermute | solution.py:51
  41.4 4.6 %collective-permute-start.1 = (bf16[128,2048]{0,1:T(8,128)(2,1)}, bf16[128,2048]{0,1:T(8,128)(2,1)S(1)}, u32[]{:S(2)}, u32[]{:S(2)}) collective-permute-start(bf16[128,2048]{0,1:T(8,128)(2,1)} %get-tuple-element.3), channel_id=1, source_target_pairs={{0,8},{4,12},{8,0},{12,4},{1,9},{5,13},{9,1},{13,5},{2,10},{6,14},... | collective-permute-start | bytes 1572872 | tf_op jit(solution)/shard_map/ppermute | solution.py:51
  46.0 3.3 %collective-permute-start.2 = (bf16[128,2048]{0,1:T(8,128)(2,1)}, bf16[128,2048]{0,1:T(8,128)(2,1)S(1)}, u32[]{:S(2)}, u32[]{:S(2)}) collective-permute-start(bf16[128,2048]{0,1:T(8,128)(2,1)} %get-tuple-element.2), channel_id=1, source_target_pairs={{0,12},{4,0},{8,4},{12,8},{1,13},{5,1},{9,5},{13,9},{2,14},{6,2},{... | collective-permute-start | bytes 1572872 | tf_op jit(solution)/shard_map/ppermute | solution.py:51
  51.7 3.4 %collective-permute-done = bf16[128,2048]{0,1:T(8,128)(2,1)S(1)} collective-permute-done((bf16[128,2048]{0,1:T(8,128)(2,1)}, bf16[128,2048]{0,1:T(8,128)(2,1)S(1)}, u32[]{:S(2)}, u32[]{:S(2)}) %collective-permute-start) | collective-permute-done | bytes 524320 | tf_op jit(solution)/shard_map/ppermute | solution.py:51
  56.0 10.7 %collective-permute-done.1 = bf16[128,2048]{0,1:T(8,128)(2,1)S(1)} collective-permute-done((bf16[128,2048]{0,1:T(8,128)(2,1)}, bf16[128,2048]{0,1:T(8,128)(2,1)S(1)}, u32[]{:S(2)}, u32[]{:S(2)}) %collective-permute-start.1) | collective-permute-done | bytes 524320 | tf_op jit(solution)/shard_map/ppermute | solution.py:51
  69.0 1.2 fusion.4
  70.3 2.7 %gather_fusion.1 = bf16[64,576,32]{1,2,0:T(8,128)(2,1)S(1)} fusion(bf16[576,64,32]{0,2,1:T(8,128)(2,1)} %fusion.4, s32[1024]{0:T(1024)S(1)} %pad_clamp_fusion), kind=kCustom, calls=%fused_computation.1 | custom fusion | bytes 4718848 | tf_op jit(solution)/shard_map/jit(_take)/gather | solution.py:62
  73.0 16.1 %all-to-all-done = bf16[16,32,512]{2,1,0:T(8,128)(2,1)S(1)} async-done(((bf16[16,32,512]{2,1,0:T(8,128)(2,1)}), bf16[16,32,512]{2,1,0:T(8,128)(2,1)S(1)}, u32[]{:S(2)}, u32[]{:S(2)}) %all-to-all-start) | async-done | bytes 524320 | tf_op jit(solution)/shard_map/all_to_all | solution.py:52
  89.1 1.9 %collective-permute-start.5 = (bf16[16,32,512]{2,1,0:T(8,128)(2,1)S(1)}, bf16[16,32,512]{2,1,0:T(8,128)(2,1)S(1)}, u32[]{:S(2)}, u32[]{:S(2)}) collective-permute-start(bf16[16,32,512]{2,1,0:T(8,128)(2,1)S(1)} %all-to-all-done), channel_id=1, source_target_pairs={{0,48},{16,32},{32,16},{48,0},{1,49},{17,33},{33,17},{49,1},{2,50}... | collective-permute-start | bytes 1572872 | tf_op jit(solution)/shard_map/ppermute | solution.py:56
  91.6 2.4 %collective-permute-start.3 = (bf16[16,32,512]{2,1,0:T(8,128)(2,1)S(1)}, bf16[16,32,512]{2,1,0:T(8,128)(2,1)S(1)}, u32[]{:S(2)}, u32[]{:S(2)}) collective-permute-start(bf16[16,32,512]{2,1,0:T(8,128)(2,1)S(1)} %all-to-all-done), channel_id=1, source_target_pairs={{0,16},{16,0},{32,48},{48,32},{1,17},{17,1},{33,49},{49,33},{2,18}... | collective-permute-start | bytes 1572872 | tf_op jit(solution)/shard_map/ppermute | solution.py:56
  94.0 4.9 %collective-permute-start.4 = (bf16[16,32,512]{2,1,0:T(8,128)(2,1)S(1)}, bf16[16,32,512]{2,1,0:T(8,128)(2,1)S(1)}, u32[]{:S(2)}, u32[]{:S(2)}) collective-permute-start(bf16[16,32,512]{2,1,0:T(8,128)(2,1)S(1)} %all-to-all-done), channel_id=1, source_target_pairs={{0,32},{16,48},{32,0},{48,16},{1,33},{17,49},{33,1},{49,17},{2,34}... | collective-permute-start | bytes 1572872 | tf_op jit(solution)/shard_map/ppermute | solution.py:56
  99.4 7.3 %collective-permute-done.5 = bf16[16,32,512]{2,1,0:T(8,128)(2,1)S(1)} collective-permute-done((bf16[16,32,512]{2,1,0:T(8,128)(2,1)S(1)}, bf16[16,32,512]{2,1,0:T(8,128)(2,1)S(1)}, u32[]{:S(2)}, u32[]{:S(2)}) %collective-permute-start.5) | collective-permute-done | bytes 524320 | tf_op jit(solution)/shard_map/ppermute | solution.py:56
  107.2 9.6 %collective-permute-done.3 = bf16[16,32,512]{2,1,0:T(8,128)(2,1)S(1)} collective-permute-done((bf16[16,32,512]{2,1,0:T(8,128)(2,1)S(1)}, bf16[16,32,512]{2,1,0:T(8,128)(2,1)S(1)}, u32[]{:S(2)}, u32[]{:S(2)}) %collective-permute-start.3) | collective-permute-done | bytes 524320 | tf_op jit(solution)/shard_map/ppermute | solution.py:56
  118.4 4.9 %collective-permute-start.6 = (f32[144,512]{1,0:T(8,128)S(1)}, f32[144,512]{1,0:T(8,128)S(1)}, u32[]{:S(2)}, u32[]{:S(2)}) collective-permute-start(f32[144,512]{1,0:T(8,128)S(1)} %get-tuple-element.11), channel_id=1, source_target_pairs={{0,8},{4,12},{8,0},{12,4},{1,9},{5,13},{9,1},{13,5},{2,10},{6,14},... | collective-permute-start | bytes 884744 | tf_op jit(solution)/shard_map/ppermute | solution.py:82
  123.3 3.0 %collective-permute-start.7 = (f32[144,512]{1,0:T(8,128)S(1)}, f32[144,512]{1,0:T(8,128)S(1)}, u32[]{:S(2)}, u32[]{:S(2)}) collective-permute-start(f32[144,512]{1,0:T(8,128)S(1)} %get-tuple-element.12), channel_id=1, source_target_pairs={{0,12},{4,0},{8,4},{12,8},{1,13},{5,1},{9,5},{13,9},{2,14},{6,2},{... | collective-permute-start | bytes 884744 | tf_op jit(solution)/shard_map/ppermute | solution.py:82
  126.4 2.8 %collective-permute-start.8 = (f32[144,512]{1,0:T(8,128)S(1)}, f32[144,512]{1,0:T(8,128)S(1)}, u32[]{:S(2)}, u32[]{:S(2)}) collective-permute-start(f32[144,512]{1,0:T(8,128)S(1)} %get-tuple-element.10), channel_id=1, source_target_pairs={{0,4},{4,8},{8,12},{12,0},{1,5},{5,9},{9,13},{13,1},{2,6},{6,10},{... | collective-permute-start | bytes 884744 | tf_op jit(solution)/shard_map/ppermute | solution.py:82
  129.2 2.1 %collective-permute-done.6 = f32[144,512]{1,0:T(8,128)S(1)} collective-permute-done((f32[144,512]{1,0:T(8,128)S(1)}, f32[144,512]{1,0:T(8,128)S(1)}, u32[]{:S(2)}, u32[]{:S(2)}) %collective-permute-start.6) | collective-permute-done | bytes 294944 | tf_op jit(solution)/shard_map/ppermute | solution.py:82
  131.3 5.9 %collective-permute-done.7 = f32[144,512]{1,0:T(8,128)S(1)} collective-permute-done((f32[144,512]{1,0:T(8,128)S(1)}, f32[144,512]{1,0:T(8,128)S(1)}, u32[]{:S(2)}, u32[]{:S(2)}) %collective-permute-start.7) | collective-permute-done | bytes 294944 | tf_op jit(solution)/shard_map/ppermute | solution.py:82
  (48 shorter events, 12.4 us)
Async XLA Ops:
  0.6 49.0 %copy-start = (s32[64]{0:T(128)S(1)}, s32[64]{0:T(128)}, u32[]{:S(2)}) copy-start(s32[64]{0:T(128)} %param.7) | copy-start | bytes 772
  3.4 85.7 %all-to-all-start = ((bf16[16,32,512]{2,1,0:T(8,128)(2,1)}), bf16[16,32,512]{2,1,0:T(8,128)(2,1)S(1)}, u32[]{:S(2)}, u32[]{:S(2)}) async-start(bf16[16,32,512]{2,1,0:T(8,128)(2,1)} %reshape.164), calls=%async_computation | async-start | bytes 1048576 | tf_op jit(solution)/shard_map/all_to_all | solution.py:52
  36.8 13.7 %copy-start.1 = (s32[8192]{0:T(1024)S(1)}, s32[8192]{0:T(1024)}, u32[]{:S(2)}) copy-start(s32[8192]{0:T(1024)} %param.8) | copy-start | bytes 98308
  38.0 17.1 %collective-permute-start = (bf16[128,2048]{0,1:T(8,128)(2,1)}, bf16[128,2048]{0,1:T(8,128)(2,1)S(1)}, u32[]{:S(2)}, u32[]{:S(2)}) collective-permute-start(bf16[128,2048]{0,1:T(8,128)(2,1)} %get-tuple-element.4), channel_id=1, source_target_pairs={{0,4},{4,8},{8,12},{12,0},{1,5},{5,9},{9,13},{13,1},{2,6},{6,10},{... | collective-permute-start | bytes 1572872 | tf_op jit(solution)/shard_map/ppermute | solution.py:51
  41.4 25.2 %collective-permute-start.1 = (bf16[128,2048]{0,1:T(8,128)(2,1)}, bf16[128,2048]{0,1:T(8,128)(2,1)S(1)}, u32[]{:S(2)}, u32[]{:S(2)}) collective-permute-start(bf16[128,2048]{0,1:T(8,128)(2,1)} %get-tuple-element.3), channel_id=1, source_target_pairs={{0,8},{4,12},{8,0},{12,4},{1,9},{5,13},{9,1},{13,5},{2,10},{6,14},... | collective-permute-start | bytes 1572872 | tf_op jit(solution)/shard_map/ppermute | solution.py:51
  46.0 22.1 %collective-permute-start.2 = (bf16[128,2048]{0,1:T(8,128)(2,1)}, bf16[128,2048]{0,1:T(8,128)(2,1)S(1)}, u32[]{:S(2)}, u32[]{:S(2)}) collective-permute-start(bf16[128,2048]{0,1:T(8,128)(2,1)} %get-tuple-element.2), channel_id=1, source_target_pairs={{0,12},{4,0},{8,4},{12,8},{1,13},{5,1},{9,5},{13,9},{2,14},{6,2},{... | collective-permute-start | bytes 1572872 | tf_op jit(solution)/shard_map/ppermute | solution.py:51
  89.1 17.6 %collective-permute-start.5 = (bf16[16,32,512]{2,1,0:T(8,128)(2,1)S(1)}, bf16[16,32,512]{2,1,0:T(8,128)(2,1)S(1)}, u32[]{:S(2)}, u32[]{:S(2)}) collective-permute-start(bf16[16,32,512]{2,1,0:T(8,128)(2,1)S(1)} %all-to-all-done), channel_id=1, source_target_pairs={{0,48},{16,32},{32,16},{48,0},{1,49},{17,33},{33,17},{49,1},{2,50}... | collective-permute-start | bytes 1572872 | tf_op jit(solution)/shard_map/ppermute | solution.py:56
  91.6 25.2 %collective-permute-start.3 = (bf16[16,32,512]{2,1,0:T(8,128)(2,1)S(1)}, bf16[16,32,512]{2,1,0:T(8,128)(2,1)S(1)}, u32[]{:S(2)}, u32[]{:S(2)}) collective-permute-start(bf16[16,32,512]{2,1,0:T(8,128)(2,1)S(1)} %all-to-all-done), channel_id=1, source_target_pairs={{0,16},{16,0},{32,48},{48,32},{1,17},{17,1},{33,49},{49,33},{2,18}... | collective-permute-start | bytes 1572872 | tf_op jit(solution)/shard_map/ppermute | solution.py:56
  94.0 23.4 %collective-permute-start.4 = (bf16[16,32,512]{2,1,0:T(8,128)(2,1)S(1)}, bf16[16,32,512]{2,1,0:T(8,128)(2,1)S(1)}, u32[]{:S(2)}, u32[]{:S(2)}) collective-permute-start(bf16[16,32,512]{2,1,0:T(8,128)(2,1)S(1)} %all-to-all-done), channel_id=1, source_target_pairs={{0,32},{16,48},{32,0},{48,16},{1,33},{17,49},{33,1},{49,17},{2,34}... | collective-permute-start | bytes 1572872 | tf_op jit(solution)/shard_map/ppermute | solution.py:56
  118.4 12.9 %collective-permute-start.6 = (f32[144,512]{1,0:T(8,128)S(1)}, f32[144,512]{1,0:T(8,128)S(1)}, u32[]{:S(2)}, u32[]{:S(2)}) collective-permute-start(f32[144,512]{1,0:T(8,128)S(1)} %get-tuple-element.11), channel_id=1, source_target_pairs={{0,8},{4,12},{8,0},{12,4},{1,9},{5,13},{9,1},{13,5},{2,10},{6,14},... | collective-permute-start | bytes 884744 | tf_op jit(solution)/shard_map/ppermute | solution.py:82
  123.3 13.8 %collective-permute-start.7 = (f32[144,512]{1,0:T(8,128)S(1)}, f32[144,512]{1,0:T(8,128)S(1)}, u32[]{:S(2)}, u32[]{:S(2)}) collective-permute-start(f32[144,512]{1,0:T(8,128)S(1)} %get-tuple-element.12), channel_id=1, source_target_pairs={{0,12},{4,0},{8,4},{12,8},{1,13},{5,1},{9,5},{13,9},{2,14},{6,2},{... | collective-permute-start | bytes 884744 | tf_op jit(solution)/shard_map/ppermute | solution.py:82
  126.4 11.5 %collective-permute-start.8 = (f32[144,512]{1,0:T(8,128)S(1)}, f32[144,512]{1,0:T(8,128)S(1)}, u32[]{:S(2)}, u32[]{:S(2)}) collective-permute-start(f32[144,512]{1,0:T(8,128)S(1)} %get-tuple-element.10), channel_id=1, source_target_pairs={{0,4},{4,8},{8,12},{12,0},{1,5},{5,9},{9,13},{13,1},{2,6},{6,10},{... | collective-permute-start | bytes 884744 | tf_op jit(solution)/shard_map/ppermute | solution.py:82

commit v8 on v7

--- a/solution.py
+++ b/solution.py
@@ -2,9 +2,39 @@
 import jax.numpy as jnp
 import numpy as np
 from jax import lax
+from jax.experimental import pallas as pl
+from jax.experimental.pallas import tpu as pltpu
 from jax.sharding import Mesh, PartitionSpec as P
 
 FSDP = ("ft", "fs")
+
+
+def combine_kernel(b0, b1, b2, b3, hidden_ref, digest_ref):
+    rows, width = hidden_ref.shape
+    total = (b0[...] + b2[...]) + (b1[...] + b3[...])
+    gate = total[:rows, :width]
+    up = total[:rows, width:]
+    hidden_ref[...] = (gate / (1.0 + jnp.exp(-gate)) * up).astype(hidden_ref.dtype)
+    digest_ref[...] = 8.0 * total[rows:, :]
+
+
+def combine(back, probe_rows, rank_width):
+    block_rows, width2 = back[0].shape
+    vmem = pl.BlockSpec(memory_space=pltpu.VMEM)
+    return pl.pallas_call(
+        combine_kernel,
+        out_shape=(
+            jax.ShapeDtypeStruct((probe_rows, rank_width), jnp.bfloat16),
+            jax.ShapeDtypeStruct((block_rows - probe_rows, width2), jnp.float32),
+        ),
+        in_specs=[vmem] * 4,
+        out_specs=(vmem, vmem),
+        cost_estimate=pl.CostEstimate(
+            flops=4 * block_rows * width2,
+            transcendentals=probe_rows * rank_width,
+            bytes_accessed=4 * 4 * block_rows * width2,
+        ),
+    )(*back)
 
 
 def on_device(trainer_gate, trainer_up, owner_map, sketch_seeds, probes):
@@ -82,18 +112,19 @@
             packed = lax.ppermute(packed, "rep", pairs)
         back.append(packed)
     if n_rep == 4:
-        summed = (back[0] + back[2]) + (back[1] + back[3])
+        hidden, digest_rows = combine(back, probe_rows, rank_width)
     else:
         slot_of = (jnp.arange(n_rep, dtype=jnp.int32) - replica) % n_rep
         pieces = jnp.take(jnp.stack(back), slot_of, axis=0)
         summed = pieces[0]
         for other in range(1, n_rep):
             summed = summed + pieces[other]
-    hidden_sum = summed[:probe_rows]
-    digest_sum = summed[probe_rows:].reshape(blocks_all, 2, narrow)
-    digest = 8.0 * digest_sum.transpose(1, 0, 2).reshape(2, blocks_all, 1, narrow)
-    hidden = jax.nn.silu(hidden_sum[:, :rank_width]) * hidden_sum[:, rank_width:]
-    hidden = hidden.astype(jnp.bfloat16)
+        hidden_sum = summed[:probe_rows]
+        digest_rows = 8.0 * summed[probe_rows:]
+        hidden = jax.nn.silu(hidden_sum[:, :rank_width]) * hidden_sum[:, rank_width:]
+        hidden = hidden.astype(jnp.bfloat16)
+    digest_sum = digest_rows.reshape(blocks_all, 2, narrow)
+    digest = digest_sum.transpose(1, 0, 2).reshape(2, blocks_all, 1, narrow)
     return (digest, hidden.reshape(1, 1, probe_rows, 1, rank_width))
 
 

time: 140 us -> 147 us (1.050)
  the two profiles are of different devices: /device:TPU:72 before, /device:TPU:64 now
where the time goes in v8:
time: 147 us; the launch traced here: 146 us
  waiting for transfers between devices  60.6 us (41%)
  starting transfers between devices  58.7 us (40%)
  local copies, waits for them, and re-layouts  16.7 us (11%)
  other arithmetic  5.43 us (4%)
  matrix products  2.02 us (1%)
  Pallas kernels  1.93 us (1%)
    all_to_all x1, starting transfers between devices, on_device(): recv = lax.all_to_all(send, 'ft', 0, 0, tiled=True)  28 us
    ppermute x3, waiting for transfers between devices, on_device(): shared.append(lax.ppermute(recv, 'fs', pairs))  16.9 us
    all_to_all x1, waiting for transfers between devices, on_device(): recv = lax.all_to_all(send, 'ft', 0, 0, tiled=True)  16.1 us
    ppermute x3, waiting for transfers between devices, on_device(): normed_got.append(lax.ppermute(chunks[k], 'rep', pairs))  14.7 us
    ppermute x3, waiting for transfers between devices, on_device(): packed = lax.ppermute(packed, 'rep', pairs)  12.8 us
    ppermute x3, starting transfers between devices, on_device(): normed_got.append(lax.ppermute(chunks[k], 'rep', pairs))  11.4 us
    ppermute x3, starting transfers between devices, on_device(): packed = lax.ppermute(packed, 'rep', pairs)  10.2 us
    ppermute x3, starting transfers between devices, on_device(): shared.append(lax.ppermute(recv, 'fs', pairs))  9.2 us
  transfers between devices with their start and end apart: 10, of which 9 were waited for; matrix products, arithmetic and copies ran while one was open for 12% of the time, Pallas kernels for 0%

profile of v8, /device:TPU:64, one launch (start us, length us, event | category | flops | bytes accessed | tf_op | source)
XLA Modules:
  0.0 146.3 jit_solution(5711444775887098151)
XLA Ops:
  2.3 1.1 reshape.165
  3.4 28.0 %all-to-all-start = ((bf16[16,32,512]{2,1,0:T(8,128)(2,1)}), bf16[16,32,512]{2,1,0:T(8,128)(2,1)S(1)}, u32[]{:S(2)}, u32[]{:S(2)}) async-start(bf16[16,32,512]{2,1,0:T(8,128)(2,1)} %reshape.165), calls=%async_computation | async-start | bytes 1048576 | tf_op jit(solution)/shard_map/all_to_all | solution.py:82
  31.4 3.2 %copy.17 = bf16[1,1,128,8192]{2,3,1,0:T(8,128)(2,1)S(1)} copy(bf16[1,1,128,8192]{3,2,1,0:T(8,128)(2,1)} %param.9) | data formatting | bytes 4194304 | tf_op args[4]
  34.6 1.1 multiply_reduce_fusion
  36.8 1.2 dynamic-slice_bitcast_fusion
  38.0 3.4 %collective-permute-start = (bf16[128,2048]{0,1:T(8,128)(2,1)}, bf16[128,2048]{0,1:T(8,128)(2,1)S(1)}, u32[]{:S(2)}, u32[]{:S(2)}) collective-permute-start(bf16[128,2048]{0,1:T(8,128)(2,1)} %get-tuple-element.8), channel_id=1, source_target_pairs={{0,4},{4,8},{8,12},{12,0},{1,5},{5,9},{9,13},{13,1},{2,6},{6,10},{... | collective-permute-start | bytes 1572872 | tf_op jit(solution)/shard_map/ppermute | solution.py:81
  41.4 4.6 %collective-permute-start.1 = (bf16[128,2048]{0,1:T(8,128)(2,1)}, bf16[128,2048]{0,1:T(8,128)(2,1)S(1)}, u32[]{:S(2)}, u32[]{:S(2)}) collective-permute-start(bf16[128,2048]{0,1:T(8,128)(2,1)} %get-tuple-element.7), channel_id=1, source_target_pairs={{0,8},{4,12},{8,0},{12,4},{1,9},{5,13},{9,1},{13,5},{2,10},{6,14},... | collective-permute-start | bytes 1572872 | tf_op jit(solution)/shard_map/ppermute | solution.py:81
  46.0 3.3 %collective-permute-start.2 = (bf16[128,2048]{0,1:T(8,128)(2,1)}, bf16[128,2048]{0,1:T(8,128)(2,1)S(1)}, u32[]{:S(2)}, u32[]{:S(2)}) collective-permute-start(bf16[128,2048]{0,1:T(8,128)(2,1)} %get-tuple-element.6), channel_id=1, source_target_pairs={{0,12},{4,0},{8,4},{12,8},{1,13},{5,1},{9,5},{13,9},{2,14},{6,2},{... | collective-permute-start | bytes 1572872 | tf_op jit(solution)/shard_map/ppermute | solution.py:81
  51.7 3.4 %collective-permute-done = bf16[128,2048]{0,1:T(8,128)(2,1)S(1)} collective-permute-done((bf16[128,2048]{0,1:T(8,128)(2,1)}, bf16[128,2048]{0,1:T(8,128)(2,1)S(1)}, u32[]{:S(2)}, u32[]{:S(2)}) %collective-permute-start) | collective-permute-done | bytes 524320 | tf_op jit(solution)/shard_map/ppermute | solution.py:81
  56.0 10.6 %collective-permute-done.1 = bf16[128,2048]{0,1:T(8,128)(2,1)S(1)} collective-permute-done((bf16[128,2048]{0,1:T(8,128)(2,1)}, bf16[128,2048]{0,1:T(8,128)(2,1)S(1)}, u32[]{:S(2)}, u32[]{:S(2)}) %collective-permute-start.1) | collective-permute-done | bytes 524320 | tf_op jit(solution)/shard_map/ppermute | solution.py:81
  69.1 1.2 fusion.4
  70.2 2.7 %gather_fusion.1 = bf16[64,576,32]{1,2,0:T(8,128)(2,1)S(1)} fusion(bf16[576,64,32]{0,2,1:T(8,128)(2,1)} %fusion.4, s32[1024]{0:T(1024)S(1)} %pad_clamp_fusion), kind=kCustom, calls=%fused_computation.1 | custom fusion | bytes 4718848 | tf_op jit(solution)/shard_map/jit(_take)/gather | solution.py:92
  73.0 16.1 %all-to-all-done = bf16[16,32,512]{2,1,0:T(8,128)(2,1)S(1)} async-done(((bf16[16,32,512]{2,1,0:T(8,128)(2,1)}), bf16[16,32,512]{2,1,0:T(8,128)(2,1)S(1)}, u32[]{:S(2)}, u32[]{:S(2)}) %all-to-all-start) | async-done | bytes 524320 | tf_op jit(solution)/shard_map/all_to_all | solution.py:82
  89.1 1.9 %collective-permute-start.5 = (bf16[16,32,512]{2,1,0:T(8,128)(2,1)S(1)}, bf16[16,32,512]{2,1,0:T(8,128)(2,1)S(1)}, u32[]{:S(2)}, u32[]{:S(2)}) collective-permute-start(bf16[16,32,512]{2,1,0:T(8,128)(2,1)S(1)} %all-to-all-done), channel_id=1, source_target_pairs={{0,48},{16,32},{32,16},{48,0},{1,49},{17,33},{33,17},{49,1},{2,50}... | collective-permute-start | bytes 1572872 | tf_op jit(solution)/shard_map/ppermute | solution.py:86
  91.6 3.5 %collective-permute-start.3 = (bf16[16,32,512]{2,1,0:T(8,128)(2,1)S(1)}, bf16[16,32,512]{2,1,0:T(8,128)(2,1)S(1)}, u32[]{:S(2)}, u32[]{:S(2)}) collective-permute-start(bf16[16,32,512]{2,1,0:T(8,128)(2,1)S(1)} %all-to-all-done), channel_id=1, source_target_pairs={{0,16},{16,0},{32,48},{48,32},{1,17},{17,1},{33,49},{49,33},{2,18}... | collective-permute-start | bytes 1572872 | tf_op jit(solution)/shard_map/ppermute | solution.py:86
  95.1 3.8 %collective-permute-start.4 = (bf16[16,32,512]{2,1,0:T(8,128)(2,1)S(1)}, bf16[16,32,512]{2,1,0:T(8,128)(2,1)S(1)}, u32[]{:S(2)}, u32[]{:S(2)}) collective-permute-start(bf16[16,32,512]{2,1,0:T(8,128)(2,1)S(1)} %all-to-all-done), channel_id=1, source_target_pairs={{0,32},{16,48},{32,0},{48,16},{1,33},{17,49},{33,1},{49,17},{2,34}... | collective-permute-start | bytes 1572872 | tf_op jit(solution)/shard_map/ppermute | solution.py:86
  99.4 7.3 %collective-permute-done.5 = bf16[16,32,512]{2,1,0:T(8,128)(2,1)S(1)} collective-permute-done((bf16[16,32,512]{2,1,0:T(8,128)(2,1)S(1)}, bf16[16,32,512]{2,1,0:T(8,128)(2,1)S(1)}, u32[]{:S(2)}, u32[]{:S(2)}) %collective-permute-start.5) | collective-permute-done | bytes 524320 | tf_op jit(solution)/shard_map/ppermute | solution.py:86
  107.2 9.6 %collective-permute-done.3 = bf16[16,32,512]{2,1,0:T(8,128)(2,1)S(1)} collective-permute-done((bf16[16,32,512]{2,1,0:T(8,128)(2,1)S(1)}, bf16[16,32,512]{2,1,0:T(8,128)(2,1)S(1)}, u32[]{:S(2)}, u32[]{:S(2)}) %collective-permute-start.3) | collective-permute-done | bytes 524320 | tf_op jit(solution)/shard_map/ppermute | solution.py:86
  119.1 4.7 %collective-permute-start.6 = (f32[144,512]{1,0:T(8,128)S(1)}, f32[144,512]{1,0:T(8,128)S(1)}, u32[]{:S(2)}, u32[]{:S(2)}) collective-permute-start(f32[144,512]{1,0:T(8,128)S(1)} %get-tuple-element.15), channel_id=1, source_target_pairs={{0,12},{4,0},{8,4},{12,8},{1,13},{5,1},{9,5},{13,9},{2,14},{6,2},{... | collective-permute-start | bytes 884744 | tf_op jit(solution)/shard_map/ppermute | solution.py:112
  123.8 2.7 %collective-permute-start.7 = (f32[144,512]{1,0:T(8,128)S(1)}, f32[144,512]{1,0:T(8,128)S(1)}, u32[]{:S(2)}, u32[]{:S(2)}) collective-permute-start(f32[144,512]{1,0:T(8,128)S(1)} %get-tuple-element.16), channel_id=1, source_target_pairs={{0,8},{4,12},{8,0},{12,4},{1,9},{5,13},{9,1},{13,5},{2,10},{6,14},... | collective-permute-start | bytes 884744 | tf_op jit(solution)/shard_map/ppermute | solution.py:112
  126.5 2.8 %collective-permute-start.8 = (f32[144,512]{1,0:T(8,128)S(1)}, f32[144,512]{1,0:T(8,128)S(1)}, u32[]{:S(2)}, u32[]{:S(2)}) collective-permute-start(f32[144,512]{1,0:T(8,128)S(1)} %get-tuple-element.14), channel_id=1, source_target_pairs={{0,4},{4,8},{8,12},{12,0},{1,5},{5,9},{9,13},{13,1},{2,6},{6,10},{... | collective-permute-start | bytes 884744 | tf_op jit(solution)/shard_map/ppermute | solution.py:112
  129.3 7.3 %collective-permute-done.6.b1 = f32[144,512]{1,0:T(8,128)S(1)} collective-permute-done((f32[144,512]{1,0:T(8,128)S(1)}, f32[144,512]{1,0:T(8,128)S(1)}, u32[]{:S(2)}, u32[]{:S(2)}) %collective-permute-start.6) | collective-permute-done | bytes 294944 | tf_op jit(solution)/shard_map/ppermute | solution.py:112
  137.1 5.0 %collective-permute-done.8.b3 = f32[144,512]{1,0:T(8,128)S(1)} collective-permute-done((f32[144,512]{1,0:T(8,128)S(1)}, f32[144,512]{1,0:T(8,128)S(1)}, u32[]{:S(2)}, u32[]{:S(2)}) %collective-permute-start.8) | collective-permute-done | bytes 294944 | tf_op jit(solution)/shard_map/ppermute | solution.py:112
  142.9 1.9 %shard_map.68 = (bf16[128,256]{1,0:T(8,128)(2,1)}, f32[16,512]{1,0:T(8,128)}) custom-call(f32[144,512]{1,0:T(8,128)} %get-tuple-element.17.b0, f32[144,512]{1,0:T(8,128)} %copy-done.1, f32[144,512]{1,0:T(8,128)} %copy-done.2, f32[144,512]{1,0:T(8,128)} %copy-done.3), custom_call_target="tpu_custom_call" | custom-call | flops 294912 | bytes 1179648 | tf_op jit(solution)/shard_map/pallas_call | solution.py:24
  (52 shorter events, 14.7 us)
Async XLA Ops:
  0.6 49.0 %copy-start = (s32[64]{0:T(128)S(1)}, s32[64]{0:T(128)}, u32[]{:S(2)}) copy-start(s32[64]{0:T(128)} %param.7) | copy-start | bytes 772
  3.4 85.7 %all-to-all-start = ((bf16[16,32,512]{2,1,0:T(8,128)(2,1)}), bf16[16,32,512]{2,1,0:T(8,128)(2,1)S(1)}, u32[]{:S(2)}, u32[]{:S(2)}) async-start(bf16[16,32,512]{2,1,0:T(8,128)(2,1)} %reshape.165), calls=%async_computation | async-start | bytes 1048576 | tf_op jit(solution)/shard_map/all_to_all | solution.py:82
  36.8 13.7 %copy-start.4 = (s32[8192]{0:T(1024)S(1)}, s32[8192]{0:T(1024)}, u32[]{:S(2)}) copy-start(s32[8192]{0:T(1024)} %param.8) | copy-start | bytes 98308
  38.0 17.1 %collective-permute-start = (bf16[128,2048]{0,1:T(8,128)(2,1)}, bf16[128,2048]{0,1:T(8,128)(2,1)S(1)}, u32[]{:S(2)}, u32[]{:S(2)}) collective-permute-start(bf16[128,2048]{0,1:T(8,128)(2,1)} %get-tuple-element.8), channel_id=1, source_target_pairs={{0,4},{4,8},{8,12},{12,0},{1,5},{5,9},{9,13},{13,1},{2,6},{6,10},{... | collective-permute-start | bytes 1572872 | tf_op jit(solution)/shard_map/ppermute | solution.py:81
  41.4 25.2 %collective-permute-start.1 = (bf16[128,2048]{0,1:T(8,128)(2,1)}, bf16[128,2048]{0,1:T(8,128)(2,1)S(1)}, u32[]{:S(2)}, u32[]{:S(2)}) collective-permute-start(bf16[128,2048]{0,1:T(8,128)(2,1)} %get-tuple-element.7), channel_id=1, source_target_pairs={{0,8},{4,12},{8,0},{12,4},{1,9},{5,13},{9,1},{13,5},{2,10},{6,14},... | collective-permute-start | bytes 1572872 | tf_op jit(solution)/shard_map/ppermute | solution.py:81
  46.0 22.1 %collective-permute-start.2 = (bf16[128,2048]{0,1:T(8,128)(2,1)}, bf16[128,2048]{0,1:T(8,128)(2,1)S(1)}, u32[]{:S(2)}, u32[]{:S(2)}) collective-permute-start(bf16[128,2048]{0,1:T(8,128)(2,1)} %get-tuple-element.6), channel_id=1, source_target_pairs={{0,12},{4,0},{8,4},{12,8},{1,13},{5,1},{9,5},{13,9},{2,14},{6,2},{... | collective-permute-start | bytes 1572872 | tf_op jit(solution)/shard_map/ppermute | solution.py:81
  89.1 17.6 %collective-permute-start.5 = (bf16[16,32,512]{2,1,0:T(8,128)(2,1)S(1)}, bf16[16,32,512]{2,1,0:T(8,128)(2,1)S(1)}, u32[]{:S(2)}, u32[]{:S(2)}) collective-permute-start(bf16[16,32,512]{2,1,0:T(8,128)(2,1)S(1)} %all-to-all-done), channel_id=1, source_target_pairs={{0,48},{16,32},{32,16},{48,0},{1,49},{17,33},{33,17},{49,1},{2,50}... | collective-permute-start | bytes 1572872 | tf_op jit(solution)/shard_map/ppermute | solution.py:86
  91.6 25.2 %collective-permute-start.3 = (bf16[16,32,512]{2,1,0:T(8,128)(2,1)S(1)}, bf16[16,32,512]{2,1,0:T(8,128)(2,1)S(1)}, u32[]{:S(2)}, u32[]{:S(2)}) collective-permute-start(bf16[16,32,512]{2,1,0:T(8,128)(2,1)S(1)} %all-to-all-done), channel_id=1, source_target_pairs={{0,16},{16,0},{32,48},{48,32},{1,17},{17,1},{33,49},{49,33},{2,18}... | collective-permute-start | bytes 1572872 | tf_op jit(solution)/shard_map/ppermute | solution.py:86
  95.1 22.3 %collective-permute-start.4 = (bf16[16,32,512]{2,1,0:T(8,128)(2,1)S(1)}, bf16[16,32,512]{2,1,0:T(8,128)(2,1)S(1)}, u32[]{:S(2)}, u32[]{:S(2)}) collective-permute-start(bf16[16,32,512]{2,1,0:T(8,128)(2,1)S(1)} %all-to-all-done), channel_id=1, source_target_pairs={{0,32},{16,48},{32,0},{48,16},{1,33},{17,49},{33,1},{49,17},{2,34}... | collective-permute-start | bytes 1572872 | tf_op jit(solution)/shard_map/ppermute | solution.py:86
  119.1 17.4 %collective-permute-start.6 = (f32[144,512]{1,0:T(8,128)S(1)}, f32[144,512]{1,0:T(8,128)S(1)}, u32[]{:S(2)}, u32[]{:S(2)}) collective-permute-start(f32[144,512]{1,0:T(8,128)S(1)} %get-tuple-element.15), channel_id=1, source_target_pairs={{0,12},{4,0},{8,4},{12,8},{1,13},{5,1},{9,5},{13,9},{2,14},{6,2},{... | collective-permute-start | bytes 884744 | tf_op jit(solution)/shard_map/ppermute | solution.py:112
  123.8 13.3 %collective-permute-start.7 = (f32[144,512]{1,0:T(8,128)S(1)}, f32[144,512]{1,0:T(8,128)S(1)}, u32[]{:S(2)}, u32[]{:S(2)}) collective-permute-start(f32[144,512]{1,0:T(8,128)S(1)} %get-tuple-element.16), channel_id=1, source_target_pairs={{0,8},{4,12},{8,0},{12,4},{1,9},{5,13},{9,1},{13,5},{2,10},{6,14},... | collective-permute-start | bytes 884744 | tf_op jit(solution)/shard_map/ppermute | solution.py:112
  126.5 15.7 %collective-permute-start.8 = (f32[144,512]{1,0:T(8,128)S(1)}, f32[144,512]{1,0:T(8,128)S(1)}, u32[]{:S(2)}, u32[]{:S(2)}) collective-permute-start(f32[144,512]{1,0:T(8,128)S(1)} %get-tuple-element.14), channel_id=1, source_target_pairs={{0,4},{4,8},{8,12},{12,0},{1,5},{5,9},{9,13},{13,1},{2,6},{6,10},{... | collective-permute-start | bytes 884744 | tf_op jit(solution)/shard_map/ppermute | solution.py:112
  136.6 5.6 %copy-start.1 = (f32[144,512]{1,0:T(8,128)}, f32[144,512]{1,0:T(8,128)S(1)}, u32[]{:S(2)}) copy-start(f32[144,512]{1,0:T(8,128)S(1)} %collective-permute-done.6.b1) | copy-start | bytes 884740
  137.1 5.1 %copy-start.2 = (f32[144,512]{1,0:T(8,128)}, f32[144,512]{1,0:T(8,128)S(1)}, u32[]{:S(2)}) copy-start(f32[144,512]{1,0:T(8,128)S(1)} %collective-permute-done.7.b2) | copy-start | bytes 884740
  142.2 0.7 copy-start.3

commit v9 on v7

--- a/solution.py
+++ b/solution.py
@@ -26,8 +26,8 @@
     weights = jnp.stack([trainer_gate.reshape(rows, width), trainer_up.reshape(rows, width)])
 
     mine = lax.dynamic_slice_in_dim(weights, replica * quarter, quarter, 1)
-    send = mine.reshape(2, n_fs, piece, n_ft, rank_width).transpose(3, 1, 2, 0, 4)
-    send = send.reshape(n_ft, n_fs * piece, 2 * rank_width)
+    send = mine.reshape(2, n_fs, piece, n_ft, rank_width).transpose(3, 0, 1, 2, 4)
+    send = send.reshape(n_ft, 2 * quarter, rank_width)
 
     probe_rows = probes.shape[2]
     wide = probes.reshape(probe_rows, total_rows).astype(jnp.float32)
@@ -63,11 +63,12 @@
     lhs = lhs.reshape(lhs_rows, n_fs, n_ft * quarter)
     partial = None
     for k in range(n_fs):
-        term = jnp.dot(
-            lhs[:, k],
-            shared[k].reshape(n_ft * quarter, 2 * rank_width),
+        term = jnp.einsum(
+            "mfq,fpqc->mpc",
+            lhs[:, k].reshape(lhs_rows, n_ft, quarter),
+            shared[k].reshape(n_ft, 2, quarter, rank_width),
             preferred_element_type=jnp.float32,
-        )
+        ).reshape(lhs_rows, 2 * rank_width)
         partial = term if partial is None else partial + term
     width2 = 2 * rank_width
     hidden_part = partial[: n_rep * probe_rows].reshape(n_rep, probe_rows, width2)

time: 140 us -> 144 us (1.029)
  the two profiles are of different devices: /device:TPU:72 before, /device:TPU:64 now
where the time goes in v9:
time: 144 us; the launch traced here: 143 us
  starting transfers between devices  59.4 us (41%)
  waiting for transfers between devices  57.5 us (40%)
  local copies, waits for them, and re-layouts  16.4 us (11%)
  other arithmetic  6.68 us (5%)
  matrix products  2.02 us (1%)
    all_to_all x1, starting transfers between devices, on_device(): recv = lax.all_to_all(send, 'ft', 0, 0, tiled=True)  28 us
    ppermute x3, waiting for transfers between devices, on_device(): shared.append(lax.ppermute(recv, 'fs', pairs))  21.3 us
    ppermute x3, waiting for transfers between devices, on_device(): normed_got.append(lax.ppermute(chunks[k], 'rep', pairs))  14.7 us
    all_to_all x1, waiting for transfers between devices, on_device(): recv = lax.all_to_all(send, 'ft', 0, 0, tiled=True)  14.4 us
    ppermute x3, starting transfers between devices, on_device(): normed_got.append(lax.ppermute(chunks[k], 'rep', pairs))  11.4 us
    ppermute x3, starting transfers between devices, on_device(): packed = lax.ppermute(packed, 'rep', pairs)  10.8 us
    ppermute x3, starting transfers between devices, on_device(): shared.append(lax.ppermute(recv, 'fs', pairs))  9.2 us
    ppermute x3, waiting for transfers between devices, on_device(): packed = lax.ppermute(packed, 'rep', pairs)  7.11 us
  transfers between devices with their start and end apart: 10, of which 10 were waited for; matrix products, arithmetic and copies ran while one was open for 14% of the time, Pallas kernels for 0%

profile of v9, /device:TPU:64, one launch (start us, length us, event | category | flops | bytes accessed | tf_op | source)
XLA Modules:
  0.0 143.0 jit_solution(12009601255140616523)
XLA Ops:
  2.6 28.0 %all-to-all-start = ((bf16[16,64,256]{2,1,0:T(8,128)(2,1)}), bf16[16,64,256]{2,1,0:T(8,128)(2,1)S(1)}, u32[]{:S(2)}, u32[]{:S(2)}) async-start(bf16[16,64,256]{2,1,0:T(8,128)(2,1)} %bitcast.20), calls=%async_computation | async-start | bytes 1048576 | tf_op jit(solution)/shard_map/all_to_all | solution.py:52
  30.6 3.2 %copy.17 = bf16[1,1,128,8192]{2,3,1,0:T(8,128)(2,1)S(1)} copy(bf16[1,1,128,8192]{3,2,1,0:T(8,128)(2,1)} %param.9) | data formatting | bytes 4194304 | tf_op args[4]
  33.8 1.1 multiply_reduce_fusion
  36.0 1.2 dynamic-slice_bitcast_fusion
  37.2 3.4 %collective-permute-start = (bf16[128,2048]{0,1:T(8,128)(2,1)}, bf16[128,2048]{0,1:T(8,128)(2,1)S(1)}, u32[]{:S(2)}, u32[]{:S(2)}) collective-permute-start(bf16[128,2048]{0,1:T(8,128)(2,1)} %get-tuple-element.8), channel_id=1, source_target_pairs={{0,4},{4,8},{8,12},{12,0},{1,5},{5,9},{9,13},{13,1},{2,6},{6,10},{... | collective-permute-start | bytes 1572872 | tf_op jit(solution)/shard_map/ppermute | solution.py:51
  40.6 4.6 %collective-permute-start.1 = (bf16[128,2048]{0,1:T(8,128)(2,1)}, bf16[128,2048]{0,1:T(8,128)(2,1)S(1)}, u32[]{:S(2)}, u32[]{:S(2)}) collective-permute-start(bf16[128,2048]{0,1:T(8,128)(2,1)} %get-tuple-element.7), channel_id=1, source_target_pairs={{0,8},{4,12},{8,0},{12,4},{1,9},{5,13},{9,1},{13,5},{2,10},{6,14},... | collective-permute-start | bytes 1572872 | tf_op jit(solution)/shard_map/ppermute | solution.py:51
  45.2 3.3 %collective-permute-start.2 = (bf16[128,2048]{0,1:T(8,128)(2,1)}, bf16[128,2048]{0,1:T(8,128)(2,1)S(1)}, u32[]{:S(2)}, u32[]{:S(2)}) collective-permute-start(bf16[128,2048]{0,1:T(8,128)(2,1)} %get-tuple-element.6), channel_id=1, source_target_pairs={{0,12},{4,0},{8,4},{12,8},{1,13},{5,1},{9,5},{13,9},{2,14},{6,2},{... | collective-permute-start | bytes 1572872 | tf_op jit(solution)/shard_map/ppermute | solution.py:51
  50.9 3.4 %collective-permute-done = bf16[128,2048]{0,1:T(8,128)(2,1)S(1)} collective-permute-done((bf16[128,2048]{0,1:T(8,128)(2,1)}, bf16[128,2048]{0,1:T(8,128)(2,1)S(1)}, u32[]{:S(2)}, u32[]{:S(2)}) %collective-permute-start) | collective-permute-done | bytes 524320 | tf_op jit(solution)/shard_map/ppermute | solution.py:51
  55.2 10.6 %collective-permute-done.1 = bf16[128,2048]{0,1:T(8,128)(2,1)S(1)} collective-permute-done((bf16[128,2048]{0,1:T(8,128)(2,1)}, bf16[128,2048]{0,1:T(8,128)(2,1)S(1)}, u32[]{:S(2)}, u32[]{:S(2)}) %collective-permute-start.1) | collective-permute-done | bytes 524320 | tf_op jit(solution)/shard_map/ppermute | solution.py:51
  68.2 1.2 fusion.4
  69.4 2.7 %gather_fusion.1 = bf16[64,576,32]{1,2,0:T(8,128)(2,1)S(1)} fusion(bf16[576,64,32]{0,2,1:T(8,128)(2,1)} %fusion.4, s32[1024]{0:T(1024)S(1)} %pad_clamp_fusion), kind=kCustom, calls=%fused_computation.1 | custom fusion | bytes 4718848 | tf_op jit(solution)/shard_map/jit(_take)/gather | solution.py:62
  72.2 1.8 %broadcast_select_fusion = bf16[576,4,512]{0,2,1:T(8,128)(2,1)} fusion(bf16[576,4,512]{0,2,1:T(8,128)(2,1)S(1)} %bitcast.90, pred[4,512]{1,0:T(4,128)(4,1)S(1)} %broadcast_in_dim.21), kind=kLoop, calls=%fused_computation.4 | loop fusion | flops 1179648 | bytes 4720640 | tf_op jit(solution)/shard_map/jit(_take)/select_n | solution.py:62
  73.9 14.4 %all-to-all-done = bf16[16,64,256]{2,1,0:T(8,128)(2,1)S(1)} async-done(((bf16[16,64,256]{2,1,0:T(8,128)(2,1)}), bf16[16,64,256]{2,1,0:T(8,128)(2,1)S(1)}, u32[]{:S(2)}, u32[]{:S(2)}) %all-to-all-start) | async-done | bytes 524320 | tf_op jit(solution)/shard_map/all_to_all | solution.py:52
  88.3 1.9 %collective-permute-start.4 = (bf16[16,64,256]{2,1,0:T(8,128)(2,1)S(1)}, bf16[16,64,256]{2,1,0:T(8,128)(2,1)S(1)}, u32[]{:S(2)}, u32[]{:S(2)}) collective-permute-start(bf16[16,64,256]{2,1,0:T(8,128)(2,1)S(1)} %all-to-all-done), channel_id=1, source_target_pairs={{0,32},{16,48},{32,0},{48,16},{1,33},{17,49},{33,1},{49,17},{2,34}... | collective-permute-start | bytes 1572872 | tf_op jit(solution)/shard_map/ppermute | solution.py:56
  90.2 4.9 %collective-permute-start.5 = (bf16[16,64,256]{2,1,0:T(8,128)(2,1)S(1)}, bf16[16,64,256]{2,1,0:T(8,128)(2,1)S(1)}, u32[]{:S(2)}, u32[]{:S(2)}) collective-permute-start(bf16[16,64,256]{2,1,0:T(8,128)(2,1)S(1)} %all-to-all-done), channel_id=1, source_target_pairs={{0,48},{16,32},{32,16},{48,0},{1,49},{17,33},{33,17},{49,1},{2,50}... | collective-permute-start | bytes 1572872 | tf_op jit(solution)/shard_map/ppermute | solution.py:56
  95.2 2.4 %collective-permute-start.3 = (bf16[16,64,256]{2,1,0:T(8,128)(2,1)S(1)}, bf16[16,64,256]{2,1,0:T(8,128)(2,1)S(1)}, u32[]{:S(2)}, u32[]{:S(2)}) collective-permute-start(bf16[16,64,256]{2,1,0:T(8,128)(2,1)S(1)} %all-to-all-done), channel_id=1, source_target_pairs={{0,16},{16,0},{32,48},{48,32},{1,17},{17,1},{33,49},{49,33},{2,18}... | collective-permute-start | bytes 1572872 | tf_op jit(solution)/shard_map/ppermute | solution.py:56
  97.5 1.9 %fusion.13 = (bf16[576,1,512]{0,2,1:T(8,128)(2,1)S(1)}, bf16[576,1,512]{0,2,1:T(8,128)(2,1)S(1)}, bf16[576,1,512]{0,2,1:T(8,128)(2,1)S(1)}, bf16[576,1,512]{0,2,1:T(8,128)(2,1)S(1)}) fusion(bf16[576,4,512]{0,2,1:T(8,128)(2,1)} %broadcast_select_fusion), kind=kLoop, calls=%fused_computation.53 | loop fusion | bytes 4718592 | tf_op jit(solution)/shard_map/slice | solution.py:68
  100.0 5.0 %collective-permute-done.4 = bf16[16,64,256]{2,1,0:T(8,128)(2,1)S(1)} collective-permute-done((bf16[16,64,256]{2,1,0:T(8,128)(2,1)S(1)}, bf16[16,64,256]{2,1,0:T(8,128)(2,1)S(1)}, u32[]{:S(2)}, u32[]{:S(2)}) %collective-permute-start.4) | collective-permute-done | bytes 524320 | tf_op jit(solution)/shard_map/ppermute | solution.py:56
  105.0 11.2 %collective-permute-done.5 = bf16[16,64,256]{2,1,0:T(8,128)(2,1)S(1)} collective-permute-done((bf16[16,64,256]{2,1,0:T(8,128)(2,1)S(1)}, bf16[16,64,256]{2,1,0:T(8,128)(2,1)S(1)}, u32[]{:S(2)}, u32[]{:S(2)}) %collective-permute-start.5) | collective-permute-done | bytes 524320 | tf_op jit(solution)/shard_map/ppermute | solution.py:56
  116.3 5.1 %collective-permute-done.3 = bf16[16,64,256]{2,1,0:T(8,128)(2,1)S(1)} collective-permute-done((bf16[16,64,256]{2,1,0:T(8,128)(2,1)S(1)}, bf16[16,64,256]{2,1,0:T(8,128)(2,1)S(1)}, u32[]{:S(2)}, u32[]{:S(2)}) %collective-permute-start.3) | collective-permute-done | bytes 524320 | tf_op jit(solution)/shard_map/ppermute | solution.py:56
  123.5 4.9 %collective-permute-start.6 = (f32[144,512]{1,0:T(8,128)S(1)}, f32[144,512]{1,0:T(8,128)S(1)}, u32[]{:S(2)}, u32[]{:S(2)}) collective-permute-start(f32[144,512]{1,0:T(8,128)S(1)} %get-tuple-element.15), channel_id=1, source_target_pairs={{0,8},{4,12},{8,0},{12,4},{1,9},{5,13},{9,1},{13,5},{2,10},{6,14},... | collective-permute-start | bytes 884744 | tf_op jit(solution)/shard_map/ppermute | solution.py:83
  128.5 3.1 %collective-permute-start.7 = (f32[144,512]{1,0:T(8,128)S(1)}, f32[144,512]{1,0:T(8,128)S(1)}, u32[]{:S(2)}, u32[]{:S(2)}) collective-permute-start(f32[144,512]{1,0:T(8,128)S(1)} %get-tuple-element.16), channel_id=1, source_target_pairs={{0,12},{4,0},{8,4},{12,8},{1,13},{5,1},{9,5},{13,9},{2,14},{6,2},{... | collective-permute-start | bytes 884744 | tf_op jit(solution)/shard_map/ppermute | solution.py:83
  131.5 2.8 %collective-permute-start.8 = (f32[144,512]{1,0:T(8,128)S(1)}, f32[144,512]{1,0:T(8,128)S(1)}, u32[]{:S(2)}, u32[]{:S(2)}) collective-permute-start(f32[144,512]{1,0:T(8,128)S(1)} %get-tuple-element.14), channel_id=1, source_target_pairs={{0,4},{4,8},{8,12},{12,0},{1,5},{5,9},{9,13},{13,1},{2,6},{6,10},{... | collective-permute-start | bytes 884744 | tf_op jit(solution)/shard_map/ppermute | solution.py:83
  134.9 5.8 %collective-permute-done.7 = f32[144,512]{1,0:T(8,128)S(1)} collective-permute-done((f32[144,512]{1,0:T(8,128)S(1)}, f32[144,512]{1,0:T(8,128)S(1)}, u32[]{:S(2)}, u32[]{:S(2)}) %collective-permute-start.7) | collective-permute-done | bytes 294944 | tf_op jit(solution)/shard_map/ppermute | solution.py:83
  (52 shorter events, 14.0 us)
Async XLA Ops:
  0.6 48.1 %copy-start = (s32[64]{0:T(128)S(1)}, s32[64]{0:T(128)}, u32[]{:S(2)}) copy-start(s32[64]{0:T(128)} %param.7) | copy-start | bytes 772
  2.6 85.7 %all-to-all-start = ((bf16[16,64,256]{2,1,0:T(8,128)(2,1)}), bf16[16,64,256]{2,1,0:T(8,128)(2,1)S(1)}, u32[]{:S(2)}, u32[]{:S(2)}) async-start(bf16[16,64,256]{2,1,0:T(8,128)(2,1)} %bitcast.20), calls=%async_computation | async-start | bytes 1048576 | tf_op jit(solution)/shard_map/all_to_all | solution.py:52
  35.9 13.7 %copy-start.1 = (s32[8192]{0:T(1024)S(1)}, s32[8192]{0:T(1024)}, u32[]{:S(2)}) copy-start(s32[8192]{0:T(1024)} %param.8) | copy-start | bytes 98308
  37.2 17.1 %collective-permute-start = (bf16[128,2048]{0,1:T(8,128)(2,1)}, bf16[128,2048]{0,1:T(8,128)(2,1)S(1)}, u32[]{:S(2)}, u32[]{:S(2)}) collective-permute-start(bf16[128,2048]{0,1:T(8,128)(2,1)} %get-tuple-element.8), channel_id=1, source_target_pairs={{0,4},{4,8},{8,12},{12,0},{1,5},{5,9},{9,13},{13,1},{2,6},{6,10},{... | collective-permute-start | bytes 1572872 | tf_op jit(solution)/shard_map/ppermute | solution.py:51
  40.6 25.2 %collective-permute-start.1 = (bf16[128,2048]{0,1:T(8,128)(2,1)}, bf16[128,2048]{0,1:T(8,128)(2,1)S(1)}, u32[]{:S(2)}, u32[]{:S(2)}) collective-permute-start(bf16[128,2048]{0,1:T(8,128)(2,1)} %get-tuple-element.7), channel_id=1, source_target_pairs={{0,8},{4,12},{8,0},{12,4},{1,9},{5,13},{9,1},{13,5},{2,10},{6,14},... | collective-permute-start | bytes 1572872 | tf_op jit(solution)/shard_map/ppermute | solution.py:51
  45.2 22.1 %collective-permute-start.2 = (bf16[128,2048]{0,1:T(8,128)(2,1)}, bf16[128,2048]{0,1:T(8,128)(2,1)S(1)}, u32[]{:S(2)}, u32[]{:S(2)}) collective-permute-start(bf16[128,2048]{0,1:T(8,128)(2,1)} %get-tuple-element.6), channel_id=1, source_target_pairs={{0,12},{4,0},{8,4},{12,8},{1,13},{5,1},{9,5},{13,9},{2,14},{6,2},{... | collective-permute-start | bytes 1572872 | tf_op jit(solution)/shard_map/ppermute | solution.py:51
  88.3 16.7 %collective-permute-start.4 = (bf16[16,64,256]{2,1,0:T(8,128)(2,1)S(1)}, bf16[16,64,256]{2,1,0:T(8,128)(2,1)S(1)}, u32[]{:S(2)}, u32[]{:S(2)}) collective-permute-start(bf16[16,64,256]{2,1,0:T(8,128)(2,1)S(1)} %all-to-all-done), channel_id=1, source_target_pairs={{0,32},{16,48},{32,0},{48,16},{1,33},{17,49},{33,1},{49,17},{2,34}... | collective-permute-start | bytes 1572872 | tf_op jit(solution)/shard_map/ppermute | solution.py:56
  90.2 26.0 %collective-permute-start.5 = (bf16[16,64,256]{2,1,0:T(8,128)(2,1)S(1)}, bf16[16,64,256]{2,1,0:T(8,128)(2,1)S(1)}, u32[]{:S(2)}, u32[]{:S(2)}) collective-permute-start(bf16[16,64,256]{2,1,0:T(8,128)(2,1)S(1)} %all-to-all-done), channel_id=1, source_target_pairs={{0,48},{16,32},{32,16},{48,0},{1,49},{17,33},{33,17},{49,1},{2,50}... | collective-permute-start | bytes 1572872 | tf_op jit(solution)/shard_map/ppermute | solution.py:56
  95.2 26.3 %collective-permute-start.3 = (bf16[16,64,256]{2,1,0:T(8,128)(2,1)S(1)}, bf16[16,64,256]{2,1,0:T(8,128)(2,1)S(1)}, u32[]{:S(2)}, u32[]{:S(2)}) collective-permute-start(bf16[16,64,256]{2,1,0:T(8,128)(2,1)S(1)} %all-to-all-done), channel_id=1, source_target_pairs={{0,16},{16,0},{32,48},{48,32},{1,17},{17,1},{33,49},{49,33},{2,18}... | collective-permute-start | bytes 1572872 | tf_op jit(solution)/shard_map/ppermute | solution.py:56
  123.5 11.4 %collective-permute-start.6 = (f32[144,512]{1,0:T(8,128)S(1)}, f32[144,512]{1,0:T(8,128)S(1)}, u32[]{:S(2)}, u32[]{:S(2)}) collective-permute-start(f32[144,512]{1,0:T(8,128)S(1)} %get-tuple-element.15), channel_id=1, source_target_pairs={{0,8},{4,12},{8,0},{12,4},{1,9},{5,13},{9,1},{13,5},{2,10},{6,14},... | collective-permute-start | bytes 884744 | tf_op jit(solution)/shard_map/ppermute | solution.py:83
  128.5 12.2 %collective-permute-start.7 = (f32[144,512]{1,0:T(8,128)S(1)}, f32[144,512]{1,0:T(8,128)S(1)}, u32[]{:S(2)}, u32[]{:S(2)}) collective-permute-start(f32[144,512]{1,0:T(8,128)S(1)} %get-tuple-element.16), channel_id=1, source_target_pairs={{0,12},{4,0},{8,4},{12,8},{1,13},{5,1},{9,5},{13,9},{2,14},{6,2},{... | collective-permute-start | bytes 884744 | tf_op jit(solution)/shard_map/ppermute | solution.py:83
  131.5 9.9 %collective-permute-start.8 = (f32[144,512]{1,0:T(8,128)S(1)}, f32[144,512]{1,0:T(8,128)S(1)}, u32[]{:S(2)}, u32[]{:S(2)}) collective-permute-start(f32[144,512]{1,0:T(8,128)S(1)} %get-tuple-element.14), channel_id=1, source_target_pairs={{0,4},{4,8},{8,12},{12,0},{1,5},{5,9},{9,13},{13,1},{2,6},{6,10},{... | collective-permute-start | bytes 884744 | tf_op jit(solution)/shard_map/ppermute | solution.py:83
